TPU v7x, 512 devices: a whole 4x4x16 slice. The times are simulated.
512 devices in a mesh: px: 32 (over y, x, core), py: 16 (over z).
Axes of the slice: x: 4, y: 4, z: 16, core: 2. Of those that a mesh axis runs over, the one named last changes fastest.
Arguments:
- currents_in: bfloat16 [64, 32, 2, 32, 512], P('px', 'py'), may hold values from -6 to 6
- rad_pattern: bfloat16 [2, 512, 512], replicated, may hold values from -0.1875 to 0.1875
- far_map: bfloat16 [512, 2048], replicated, may hold values from -0.25 to 0.25
- reflect: float32 [64, 32, 512], P('px', 'py'), may hold values from 0.2 to 0.7
- centres: float32 [3, 64, 32], P(None, 'px', 'py'), may hold values from -30 to 30
- spectral_dirs: float32 [3, 512], replicated, may hold values from -3 to 3
- receiver_dirs: float32 [3, 2048], replicated, may hold values from -3 to 3
- partners: int32 [64, 32, 12], P('px', 'py'), may hold values from 0 to 2047, as said below
- partner_count: int32 [64, 32], P('px', 'py'), may hold values from 1 to 12, as said below
- pair_weight: bfloat16 [64, 32, 12], P('px', 'py'), may hold values from 0.29882812 to 1
Outputs:
- currents: bfloat16 [64, 32, 2, 32, 512], P('px', 'py')
- isar_image: float32 [32, 2048], P('py', 'px')
Inputs may be any that keep to these rules, and one draw needn't show every extreme that they name: `partners`: the first partner_count entries of a patch's list are distinct patches other than itself, at most 1 patch rows away along the hull and, counting columns around the girth (column indices wrap modulo 32), at most 2 columns away; later entries are valid patch ids that are ignored. `partner_count`: some patch lists 12 partners.
All inputs are finite; a program needn't handle non-finite values.
Results may differ from a plain program's by a relative error of at most 0.019.
Values may be sent and summed in bfloat16 or wider, within the bound.
A program may use at most 64 MiB of HBM per device.

v0:
```python
import math

import jax
import jax.numpy as jnp
from jax import lax
from jax.sharding import PartitionSpec as P

SLOTS = 12
COL_REACH = 2


def padded(block, sides, width, periodic):
    for axis, dim in sides:
        count = lax.axis_size(axis)
        forward = [(i, i + 1) for i in range(count - 1)]
        if periodic:
            forward.append((count - 1, 0))
        backward = [(target, source) for source, target in forward]
        low = lax.ppermute(
            lax.slice_in_dim(block, block.shape[dim] - width, None, axis=dim), axis, forward
        )
        high = lax.ppermute(lax.slice_in_dim(block, 0, width, axis=dim), axis, backward)
        block = jnp.concatenate([low, block, high], axis=dim)
    return block


def split_up(value, dim, size):
    dims = value.shape
    blocks = value.reshape(*dims[:dim], size, dims[dim] // size, *dims[dim + 1 :])
    return jnp.moveaxis(blocks, dim, 0)


def sum_at_owner(value, axis, dim):
    blocks = split_up(value, dim, lax.axis_size(axis))
    arrived = lax.all_to_all(blocks, axis, split_axis=0, concat_axis=0, tiled=True)
    return arrived.astype(jnp.float32).sum(axis=0)


def copy_for_each(value, axis):
    copies = jnp.broadcast_to(value, (lax.axis_size(axis), *value.shape))
    return lax.all_to_all(copies, axis, split_axis=0, concat_axis=0, tiled=True)


def over_copies(value, axis):
    everything = copy_for_each(value, axis)
    return jnp.sum(everything.astype(jnp.float32), axis=0)


def combined(rad_pattern):
    upper = jnp.concatenate([rad_pattern[0], rad_pattern[1]], axis=1)
    lower = jnp.concatenate([-rad_pattern[1], rad_pattern[0]], axis=1)
    return jnp.concatenate([upper, lower], axis=0)


def radiate(currents, rad_big):
    row_count, col_count, _, illum_count, unit_count = currents.shape
    stacked = jnp.concatenate([currents[:, :, 0], currents[:, :, 1]], axis=-1)
    flat_rows = stacked.reshape(row_count * col_count * illum_count, 2 * unit_count)
    spectra = jnp.dot(flat_rows, rad_big, preferred_element_type=jnp.float32)
    return spectra.reshape(row_count, col_count, illum_count, -1)


def receive(arriving, rad_big):
    row_count, col_count, illum_count, double = arriving.shape
    flat_rows = arriving.reshape(-1, double)
    answer = lax.dot_general(
        flat_rows, rad_big, (((1,), (1,)), ((), ())), preferred_element_type=jnp.float32
    )
    return answer.reshape(row_count, col_count, illum_count, -1)


def partner_sum(halo_flat, slot_index, weights):
    height = halo_flat.shape[0]
    onehot = slot_index[:, :, None] == jnp.arange(height, dtype=jnp.int32)[None, None, :]
    coef = jnp.sum(jnp.where(onehot, weights[:, :, None].astype(jnp.float32), 0.0), axis=1).astype(
        jnp.bfloat16
    )
    return jnp.dot(coef, halo_flat, preferred_element_type=jnp.float32)


def bounce(current_now, currents_in, rad_big, reflect, cosine, sine_part, plan):
    row_count, col_count, _, illum_count, unit_count = current_now.shape
    spectra = radiate(current_now, rad_big)
    half_width = spectra.shape[-1] // 2
    spec_re = spectra[..., :half_width]
    spec_im = spectra[..., half_width:]
    out_re = spec_re * cosine + spec_im * sine_part
    out_im = spec_im * cosine - spec_re * sine_part
    outgoing = jnp.stack([out_re, out_im], axis=2).astype(jnp.bfloat16)
    girth_block = padded(outgoing, (("py", 1),), COL_REACH, True)
    own_index, own_weights, edge_index, edge_weights, edge_count = plan
    girth_flat = girth_block.reshape(-1, 2 * illum_count * half_width)
    collected = partner_sum(girth_flat, own_index, own_weights)
    collected = collected.reshape(row_count, col_count, 2, illum_count, half_width)
    pushed = partner_sum(girth_flat, edge_index, edge_weights)
    pushed = pushed.reshape(2, col_count, 2, illum_count, half_width)
    arrived = padded(pushed, (("px", 0),), 1, False)
    collected = collected.at[0].add(arrived[0])
    collected = collected.at[row_count - 1].add(arrived[3])
    col_re = collected[:, :, 0]
    col_im = collected[:, :, 1]
    arr_re = col_re * cosine - col_im * sine_part
    arr_im = col_re * sine_part + col_im * cosine
    arriving = jnp.concatenate([arr_re, -arr_im], axis=-1).astype(jnp.bfloat16)
    answer = receive(arriving, rad_big)
    received = jnp.stack([answer[..., :unit_count], -answer[..., unit_count:]], axis=2)
    updated = currents_in.astype(jnp.float32) + reflect[:, :, None, None, :] * received
    return updated.astype(jnp.bfloat16)


def local(
    currents_in,
    rad_pattern,
    far_map,
    reflect,
    centres,
    spectral_dirs,
    receiver_dirs,
    partners,
    partner_count,
    pair_weight,
):
    row_count, col_count = partner_count.shape
    high = lax.Precision.HIGHEST
    rad_big = combined(rad_pattern)
    phi = jnp.einsum("dm,dab->abm", spectral_dirs, centres, precision=high)
    cosine = jnp.cos(phi)[:, :, None, :]
    sine_part = jnp.sin(phi)[:, :, None, :]
    total_cols = col_count * lax.axis_size("py")
    total_rows = row_count * lax.axis_size("px")
    base_row = lax.axis_index("px") * row_count
    base_col = lax.axis_index("py") * col_count
    across = col_count + 2 * COL_REACH
    local_col = jnp.arange(col_count, dtype=jnp.int32)[None, :, None]
    live = jnp.arange(SLOTS, dtype=jnp.int32)[None, None, :] < partner_count[:, :, None]
    masked_weight = jnp.where(live, pair_weight, jnp.zeros_like(pair_weight))

    def locate(lists):
        part_row = lists // total_cols
        part_col = lists % total_cols
        near_row = part_row - base_row
        near_col = (part_col - base_col - local_col + COL_REACH) % total_cols + local_col
        return (near_row, near_col)

    near_row, near_col = locate(partners)
    inside = (near_row >= 0) & (near_row < row_count)
    own_index = (jnp.clip(near_row, 0, row_count - 1) * across + near_col).reshape(
        row_count * col_count, SLOTS
    )
    own_weights = jnp.where(inside, masked_weight, jnp.zeros_like(masked_weight)).reshape(
        row_count * col_count, SLOTS
    )
    edge_ids = jnp.concatenate([partners[:1], partners[row_count - 1 :]], axis=0)
    edge_mass = jnp.concatenate([masked_weight[:1], masked_weight[row_count - 1 :]], axis=0)
    got_ids = padded(edge_ids, (("px", 0),), 1, False)
    got_mass = padded(edge_mass, (("px", 0),), 1, False)
    their_ids = jnp.stack([got_ids[0], got_ids[3]])
    their_mass = jnp.stack([got_mass[0], got_mass[3]])
    edge_row, edge_col = locate(their_ids)
    edge_inside = (edge_row >= 0) & (edge_row < row_count)
    edge_index = (jnp.clip(edge_row, 0, row_count - 1) * across + edge_col).reshape(
        2 * col_count, SLOTS
    )
    edge_weights = jnp.where(edge_inside, their_mass, jnp.zeros_like(their_mass)).reshape(
        2 * col_count, SLOTS
    )
    edge_count = jnp.full((2, col_count), SLOTS, jnp.int32)
    plan = (own_index, own_weights, edge_index, edge_weights, edge_count)
    current_now = currents_in
    for bounce_id in range(2):
        current_now = bounce(current_now, currents_in, rad_big, reflect, cosine, sine_part, plan)
    spectra = radiate(current_now, rad_big).astype(jnp.bfloat16)
    illum_count = spectra.shape[2]
    dir_count = far_map.shape[0]
    rcv_count = far_map.shape[1]
    beams = jnp.dot(spectra.reshape(-1, dir_count), far_map, preferred_element_type=jnp.float32)
    beams = beams.reshape(row_count, col_count, illum_count, 2, rcv_count)
    view = jnp.einsum("dr,dab->abr", receiver_dirs, centres, precision=high)
    cos_view = jnp.cos(view)[:, :, None, :]
    sin_view = jnp.sin(view)[:, :, None, :]
    beam_re = beams[:, :, :, 0]
    beam_im = beams[:, :, :, 1]
    far_re = jnp.sum(beam_re * cos_view - beam_im * sin_view, axis=(0, 1))
    far_im = jnp.sum(beam_re * sin_view + beam_im * cos_view, axis=(0, 1))
    factor = 1.0 / math.sqrt(total_rows * total_cols)
    far_part = jnp.stack([far_re, far_im]) * factor
    owned_far = over_copies(
        sum_at_owner(far_part.astype(jnp.bfloat16), "py", 1).astype(jnp.bfloat16), "px"
    ).astype(jnp.float32)
    bin_width = rcv_count // lax.axis_size("px")
    rcv_ids = jnp.arange(rcv_count, dtype=jnp.int32)[:, None]
    bin_ids = lax.axis_index("px") * bin_width + jnp.arange(bin_width, dtype=jnp.int32)[None, :]
    turn_angle = (rcv_ids * bin_ids % rcv_count).astype(jnp.float32) * (2.0 * math.pi / rcv_count)
    norm_factor = 1.0 / math.sqrt(rcv_count)
    cos_table = jnp.cos(turn_angle) * norm_factor
    sin_table = jnp.sin(turn_angle) * norm_factor
    image_re = jnp.dot(owned_far[0], cos_table, precision=high) + jnp.dot(
        owned_far[1], sin_table, precision=high
    )
    image_im = jnp.dot(owned_far[1], cos_table, precision=high) - jnp.dot(
        owned_far[0], sin_table, precision=high
    )
    isar_image = 0.125 * (image_re * image_re + image_im * image_im)
    return (current_now, isar_image)


def solution(mesh):
    in_specs = (
        P("px", "py", None, None, None),
        P(),
        P(),
        P("px", "py", None),
        P(None, "px", "py"),
        P(),
        P(),
        P("px", "py", None),
        P("px", "py"),
        P("px", "py", None),
    )
    out_specs = (P("px", "py", None, None, None), P("py", "px"))
    return jax.shard_map(local, mesh=mesh, in_specs=in_specs, out_specs=out_specs, check_vma=False)
```

profile of v0, /device:TPU:1, one launch (start us, length us, event | category | flops | bytes accessed | tf_op | source)
XLA Modules:
  0.0 147.0 jit_solution(5613950498323659397)
XLA Ops:
  0.7 1.2 fusion.111
  1.9 1.5 slice_bitcast_fusion.2
  4.5 11.9 %collective-permute-start.1 = (bf16[2,2,2,32,512]{4,3,1,0,2:T(8,128)(2,1)S(1)}, bf16[2,2,2,32,512]{4,3,1,0,2:T(8,128)(2,1)S(1)}, u32[]{:S(2)}, u32[]{:S(2)}) collective-permute-start(bf16[2,2,2,32,512]{4,3,1,0,2:T(8,128)(2,1)S(1)} %pad_maximum_fusion.2), channel_id=1, source_target_pairs={{1,0},{2,1},{3,2},{4,3},{5,4},{6,5},{7,6},{8,7},{9,8},{10,9},{11,1... | collective-permute-start | bytes 786440 | tf_op jit(solution)/shard_map/ppermute | solution.py:22
  16.5 1.9 %collective-permute-start = (bf16[2,2,2,32,512]{4,3,1,0,2:T(8,128)(2,1)S(1)}, bf16[2,2,2,32,512]{4,3,1,0,2:T(8,128)(2,1)S(1)}, u32[]{:S(2)}, u32[]{:S(2)}) collective-permute-start(bf16[2,2,2,32,512]{4,3,1,0,2:T(8,128)(2,1)S(1)} %pad_maximum_fusion.2), channel_id=1, source_target_pairs={{0,1},{1,2},{2,3},{3,4},{4,5},{5,6},{6,7},{7,8},{8,9},{9,10},{10,1... | collective-permute-start | bytes 786440 | tf_op jit(solution)/shard_map/ppermute | solution.py:19
  18.5 4.0 %collective-permute-start.4 = (bf16[1,2,12]{2,1,0:T(2,128)(2,1)S(1)}, bf16[1,2,12]{2,1,0:T(2,128)(2,1)S(1)}, u32[]{:S(2)}, u32[]{:S(2)}) collective-permute-start(bf16[1,2,12]{2,1,0:T(2,128)(2,1)S(1)} %get-tuple-element.98), channel_id=1, source_target_pairs={{0,16},{16,32},{32,48},{48,64},{64,80},{80,96},{96,112},{112,128},... | collective-permute-start | bytes 152 | tf_op jit(solution)/shard_map/ppermute | solution.py:19
  22.5 1.9 %collective-permute-start.5 = (bf16[1,2,12]{2,1,0:T(2,128)(2,1)S(1)}, bf16[1,2,12]{2,1,0:T(2,128)(2,1)S(1)}, u32[]{:S(2)}, u32[]{:S(2)}) collective-permute-start(bf16[1,2,12]{2,1,0:T(2,128)(2,1)S(1)} %get-tuple-element.99), channel_id=1, source_target_pairs={{16,0},{32,16},{48,32},{64,48},{80,64},{96,80},{112,96},{128,112},... | collective-permute-start | bytes 152 | tf_op jit(solution)/shard_map/ppermute | solution.py:22
  24.4 3.6 %collective-permute-start.2 = (s32[1,2,12]{2,1,0:T(2,128)S(1)}, s32[1,2,12]{2,1,0:T(2,128)S(1)}, u32[]{:S(2)}, u32[]{:S(2)}) collective-permute-start(s32[1,2,12]{2,1,0:T(2,128)S(1)} %get-tuple-element.96), channel_id=1, source_target_pairs={{0,16},{16,32},{32,48},{48,64},{64,80},{80,96},{96,112},{112,128},... | collective-permute-start | bytes 296 | tf_op jit(solution)/shard_map/ppermute | solution.py:19
  28.5 1.9 %collective-permute-start.3 = (s32[1,2,12]{2,1,0:T(2,128)S(1)}, s32[1,2,12]{2,1,0:T(2,128)S(1)}, u32[]{:S(2)}, u32[]{:S(2)}) collective-permute-start(s32[1,2,12]{2,1,0:T(2,128)S(1)} %get-tuple-element.97), channel_id=1, source_target_pairs={{16,0},{32,16},{48,32},{64,48},{80,64},{96,80},{112,96},{128,112},... | collective-permute-start | bytes 296 | tf_op jit(solution)/shard_map/ppermute | solution.py:22
  30.5 2.9 %collective-permute-done.3 = s32[1,2,12]{2,1,0:T(2,128)S(1)} collective-permute-done((s32[1,2,12]{2,1,0:T(2,128)S(1)}, s32[1,2,12]{2,1,0:T(2,128)S(1)}, u32[]{:S(2)}, u32[]{:S(2)}) %collective-permute-start.3) | collective-permute-done | bytes 128 | tf_op jit(solution)/shard_map/ppermute | solution.py:22
  33.9 1.0 copy.108
  34.9 1.6 %reshape.381 = bf16[12,32768]{1,0:T(8,128)(2,1)S(1)} reshape(bf16[2,6,2,32,512]{4,3,2,1,0:T(8,128)(2,1)} %copy.108) | data formatting | bytes 1572864 | tf_op jit(solution)/shard_map/reshape | solution.py:92
  37.1 2.0 %collective-permute-start.6 = (f32[1,2,2,32,512]{4,3,1,0,2:T(8,128)S(1)}, f32[1,2,2,32,512]{4,3,1,0,2:T(8,128)S(1)}, u32[]{:S(2)}, u32[]{:S(2)}) collective-permute-start(f32[1,2,2,32,512]{4,3,1,0,2:T(8,128)S(1)} %copy.113), channel_id=1, source_target_pairs={{0,16},{16,32},{32,48},{48,64},{64,80},{80,96},{96,112},{112,128},... | collective-permute-start | bytes 786440 | tf_op jit(solution)/shard_map/ppermute | solution.py:19
  39.1 2.4 %collective-permute-start.7 = (f32[1,2,2,32,512]{4,3,1,0,2:T(8,128)S(1)}, f32[1,2,2,32,512]{4,3,1,0,2:T(8,128)S(1)}, u32[]{:S(2)}, u32[]{:S(2)}) collective-permute-start(f32[1,2,2,32,512]{4,3,1,0,2:T(8,128)S(1)} %copy.115), channel_id=1, source_target_pairs={{16,0},{32,16},{48,32},{64,48},{80,64},{96,80},{112,96},{128,112},... | collective-permute-start | bytes 786440 | tf_op jit(solution)/shard_map/ppermute | solution.py:22
  42.6 4.1 %collective-permute-done.7 = f32[1,2,2,32,512]{4,3,1,0,2:T(8,128)S(1)} collective-permute-done((f32[1,2,2,32,512]{4,3,1,0,2:T(8,128)S(1)}, f32[1,2,2,32,512]{4,3,1,0,2:T(8,128)S(1)}, u32[]{:S(2)}, u32[]{:S(2)}) %collective-permute-start.7) | collective-permute-done | bytes 262176 | tf_op jit(solution)/shard_map/ppermute | solution.py:22
  47.0 0.8 fusion.43
  48.5 4.9 %collective-permute-start.9 = (bf16[2,2,2,32,512]{4,3,1,0,2:T(8,128)(2,1)S(1)}, bf16[2,2,2,32,512]{4,3,1,0,2:T(8,128)(2,1)S(1)}, u32[]{:S(2)}, u32[]{:S(2)}) collective-permute-start(bf16[2,2,2,32,512]{4,3,1,0,2:T(8,128)(2,1)S(1)} %pad_maximum_fusion.3), channel_id=1, source_target_pairs={{1,0},{2,1},{3,2},{4,3},{5,4},{6,5},{7,6},{8,7},{9,8},{10,9},{11,1... | collective-permute-start | bytes 786440 | tf_op jit(solution)/shard_map/ppermute | solution.py:22
  53.4 1.9 %collective-permute-start.8 = (bf16[2,2,2,32,512]{4,3,1,0,2:T(8,128)(2,1)S(1)}, bf16[2,2,2,32,512]{4,3,1,0,2:T(8,128)(2,1)S(1)}, u32[]{:S(2)}, u32[]{:S(2)}) collective-permute-start(bf16[2,2,2,32,512]{4,3,1,0,2:T(8,128)(2,1)S(1)} %pad_maximum_fusion.3), channel_id=1, source_target_pairs={{0,1},{1,2},{2,3},{3,4},{4,5},{5,6},{6,7},{7,8},{8,9},{9,10},{10,1... | collective-permute-start | bytes 786440 | tf_op jit(solution)/shard_map/ppermute | solution.py:19
  56.7 5.0 %collective-permute-done.8 = bf16[2,2,2,32,512]{4,3,1,0,2:T(8,128)(2,1)S(1)} collective-permute-done((bf16[2,2,2,32,512]{4,3,1,0,2:T(8,128)(2,1)S(1)}, bf16[2,2,2,32,512]{4,3,1,0,2:T(8,128)(2,1)S(1)}, u32[]{:S(2)}, u32[]{:S(2)}) %collective-permute-start.8) | collective-permute-done | bytes 262176 | tf_op jit(solution)/shard_map/ppermute | solution.py:19
  61.8 1.0 copy.116
  62.8 1.6 %reshape.382 = bf16[12,32768]{1,0:T(8,128)(2,1)S(1)} reshape(bf16[2,6,2,32,512]{4,3,2,1,0:T(8,128)(2,1)} %copy.116) | data formatting | bytes 1572864 | tf_op jit(solution)/shard_map/reshape | solution.py:92
  65.0 5.5 %collective-permute-start.10 = (f32[1,2,2,32,512]{4,3,1,0,2:T(8,128)S(1)}, f32[1,2,2,32,512]{4,3,1,0,2:T(8,128)S(1)}, u32[]{:S(2)}, u32[]{:S(2)}) collective-permute-start(f32[1,2,2,32,512]{4,3,1,0,2:T(8,128)S(1)} %copy.119), channel_id=1, source_target_pairs={{0,16},{16,32},{32,48},{48,64},{64,80},{80,96},{96,112},{112,128},... | collective-permute-start | bytes 786440 | tf_op jit(solution)/shard_map/ppermute | solution.py:19
  70.5 1.9 %collective-permute-start.11 = (f32[1,2,2,32,512]{4,3,1,0,2:T(8,128)S(1)}, f32[1,2,2,32,512]{4,3,1,0,2:T(8,128)S(1)}, u32[]{:S(2)}, u32[]{:S(2)}) collective-permute-start(f32[1,2,2,32,512]{4,3,1,0,2:T(8,128)S(1)} %copy.121), channel_id=1, source_target_pairs={{16,0},{32,16},{48,32},{64,48},{80,64},{96,80},{112,96},{128,112},... | collective-permute-start | bytes 786440 | tf_op jit(solution)/shard_map/ppermute | solution.py:22
  73.9 4.3 %collective-permute-done.11 = f32[1,2,2,32,512]{4,3,1,0,2:T(8,128)S(1)} collective-permute-done((f32[1,2,2,32,512]{4,3,1,0,2:T(8,128)S(1)}, f32[1,2,2,32,512]{4,3,1,0,2:T(8,128)S(1)}, u32[]{:S(2)}, u32[]{:S(2)}) %collective-permute-start.11) | collective-permute-done | bytes 262176 | tf_op jit(solution)/shard_map/ppermute | solution.py:22
  78.4 0.8 fusion.51
  81.5 21.1 %all_to_all.10 = bf16[16,2,2,2048]{3,2,1,0:T(2,128)(2,1)S(1)} all-to-all(bf16[16,2,2,2048]{3,2,1,0:T(2,128)(2,1)S(1)} %fusion.58), channel_id=1, replica_groups=mesh['px'=32,'py'=16] {'py'}, dimensions={0} | all-to-all | bytes 524288 | tf_op jit(solution)/shard_map/all_to_all | solution.py:35
  102.8 1.3 broadcast_in_dim.47
  104.1 12.6 %all-to-all-start.1 = ((bf16[32,2,2,2048]{3,2,1,0:T(2,128)(2,1)}), bf16[32,2,2,2048]{3,2,1,0:T(2,128)(2,1)S(1)}, u32[]{:S(2)}, u32[]{:S(2)}) async-start(bf16[32,2,2,2048]{3,2,1,0:T(2,128)(2,1)} %broadcast_in_dim.47), calls=%async_computation.1 | async-start | bytes 1048576 | tf_op jit(solution)/shard_map/all_to_all | solution.py:41
  117.5 10.5 %all-to-all-done.1 = bf16[32,2,2,2048]{3,2,1,0:T(2,128)(2,1)S(1)} async-done(((bf16[32,2,2,2048]{3,2,1,0:T(2,128)(2,1)}), bf16[32,2,2,2048]{3,2,1,0:T(2,128)(2,1)S(1)}, u32[]{:S(2)}, u32[]{:S(2)}) %all-to-all-start.1) | async-done | bytes 524320 | tf_op jit(solution)/shard_map/all_to_all | solution.py:41
  128.3 4.5 %fusion.18 = f32[2,64]{1,0:T(2,128)S(1)} fusion(s32[64]{0:T(128)S(1)} %iota_add_fusion, f32[2,2,2048]{2,1,0:T(2,128)S(1)} %convert_reduce_fusion), kind=kOutput, calls=%fused_computation.32 | convolution fusion | flops 5111808 | bytes 17408 | tf_op jit(solution)/shard_map/dot_general | solution.py:200
  132.8 4.5 %fusion.19 = f32[2,64]{1,0:T(2,128)S(1)} fusion(s32[64]{0:T(128)S(1)} %iota_add_fusion, f32[2,2,2048]{2,1,0:T(2,128)S(1)} %convert_reduce_fusion), kind=kOutput, calls=%fused_computation.33 | convolution fusion | flops 5111808 | bytes 17408 | tf_op jit(solution)/shard_map/dot_general | solution.py:197
  137.2 4.7 %fusion.2 = f32[2,64]{1,0:T(2,128)S(1)} fusion(f32[2,64]{1,0:T(2,128)S(1)} %fusion.18, s32[64]{0:T(128)S(1)} %iota_add_fusion, f32[2,2,2048]{2,1,0:T(2,128)S(1)} %convert_reduce_fusion), kind=kOutput, calls=%fused_computation.8 | convolution fusion | flops 5112064 | bytes 18432 | tf_op jit(solution)/shard_map/dot_general | solution.py:200
  142.0 5.1 %fusion.5 = f32[2,64]{1,0:T(2,128)} fusion(f32[2,64]{1,0:T(2,128)S(1)} %fusion.2, f32[2,64]{1,0:T(2,128)S(1)} %fusion.19, s32[64]{0:T(128)S(1)} %iota_add_fusion, f32[2,2,2048]{2,1,0:T(2,128)S(1)} %convert_reduce_fusion), kind=kOutput, calls=%fused_computation.12 | convolution fusion | flops 5112320 | bytes 19456 | tf_op jit(solution)/shard_map/dot_general | solution.py:197
  (113 shorter events, 11.8 us)
Async XLA Ops:
  0.6 79.1 %copy-start = (bf16[512,2048]{1,0:T(8,128)(2,1)S(1)}, bf16[512,2048]{1,0:T(8,128)(2,1)}, u32[]{:S(2)}) copy-start(bf16[512,2048]{1,0:T(8,128)(2,1)} %param.20) | copy-start | bytes 6291460
  0.6 2.7 %copy-start.1 = (bf16[2,2,2,32,512]{4,3,2,1,0:T(8,128)(2,1)S(1)}, bf16[2,2,2,32,512]{4,3,2,1,0:T(8,128)(2,1)}, u32[]{:S(2)}) copy-start(bf16[2,2,2,32,512]{4,3,2,1,0:T(8,128)(2,1)} %param.18) | copy-start | bytes 786436
  0.7 2.8 %copy-start.17 = (f32[3,2,2]{0,2,1:T(2,128)S(1)}, f32[3,2,2]{0,2,1:T(2,128)}, u32[]{:S(2)}) copy-start(f32[3,2,2]{0,2,1:T(2,128)} %param.22) | copy-start | bytes 148
  0.7 2.8 %copy-start.16 = (f32[3,512]{1,0:T(4,128)S(1)}, f32[3,512]{1,0:T(4,128)}, u32[]{:S(2)}) copy-start(f32[3,512]{1,0:T(4,128)} %param.23) | copy-start | bytes 18436
  1.9 2.3 %copy-start.2 = (bf16[512,512]{1,0:T(8,128)(2,1)}, bf16[512,512]{1,0:T(8,128)(2,1)S(1)}, u32[]{:S(2)}) copy-start(bf16[512,512]{1,0:T(8,128)(2,1)S(1)} %fusion.111) | copy-start | bytes 1572868
  3.4 0.8 copy-start.5
  3.4 1.0 copy-start.8
  3.7 14.7 %copy-start.12 = (s32[2,2,12]{2,1,0:T(2,128)S(1)}, s32[2,2,12]{2,1,0:T(2,128)}, u32[]{:S(2)}) copy-start(s32[2,2,12]{2,1,0:T(2,128)} %param.25) | copy-start | bytes 580
  3.8 14.7 %copy-start.13 = (bf16[2,2,12]{2,1,0:T(2,128)(2,1)S(1)}, bf16[2,2,12]{2,1,0:T(2,128)(2,1)}, u32[]{:S(2)}) copy-start(bf16[2,2,12]{2,1,0:T(2,128)(2,1)} %param.27) | copy-start | bytes 292
  3.8 14.7 %copy-start.14 = (s32[2,2]{1,0:T(2,128)S(1)}, s32[2,2]{1,0:T(2,128)}, u32[]{:S(2)}) copy-start(s32[2,2]{1,0:T(2,128)} %param.26) | copy-start | bytes 52
  4.5 29.3 %collective-permute-start.1 = (bf16[2,2,2,32,512]{4,3,1,0,2:T(8,128)(2,1)S(1)}, bf16[2,2,2,32,512]{4,3,1,0,2:T(8,128)(2,1)S(1)}, u32[]{:S(2)}, u32[]{:S(2)}) collective-permute-start(bf16[2,2,2,32,512]{4,3,1,0,2:T(8,128)(2,1)S(1)} %pad_maximum_fusion.2), channel_id=1, source_target_pairs={{1,0},{2,1},{3,2},{4,3},{5,4},{6,5},{7,6},{8,7},{9,8},{10,9},{11,1... | collective-permute-start | bytes 786440 | tf_op jit(solution)/shard_map/ppermute | solution.py:22
  16.5 17.3 %collective-permute-start = (bf16[2,2,2,32,512]{4,3,1,0,2:T(8,128)(2,1)S(1)}, bf16[2,2,2,32,512]{4,3,1,0,2:T(8,128)(2,1)S(1)}, u32[]{:S(2)}, u32[]{:S(2)}) collective-permute-start(bf16[2,2,2,32,512]{4,3,1,0,2:T(8,128)(2,1)S(1)} %pad_maximum_fusion.2), channel_id=1, source_target_pairs={{0,1},{1,2},{2,3},{3,4},{4,5},{5,6},{6,7},{7,8},{8,9},{9,10},{10,1... | collective-permute-start | bytes 786440 | tf_op jit(solution)/shard_map/ppermute | solution.py:19
  18.5 9.9 %collective-permute-start.4 = (bf16[1,2,12]{2,1,0:T(2,128)(2,1)S(1)}, bf16[1,2,12]{2,1,0:T(2,128)(2,1)S(1)}, u32[]{:S(2)}, u32[]{:S(2)}) collective-permute-start(bf16[1,2,12]{2,1,0:T(2,128)(2,1)S(1)} %get-tuple-element.98), channel_id=1, source_target_pairs={{0,16},{16,32},{32,48},{48,64},{64,80},{80,96},{96,112},{112,128},... | collective-permute-start | bytes 152 | tf_op jit(solution)/shard_map/ppermute | solution.py:19
  22.5 7.9 %collective-permute-start.5 = (bf16[1,2,12]{2,1,0:T(2,128)(2,1)S(1)}, bf16[1,2,12]{2,1,0:T(2,128)(2,1)S(1)}, u32[]{:S(2)}, u32[]{:S(2)}) collective-permute-start(bf16[1,2,12]{2,1,0:T(2,128)(2,1)S(1)} %get-tuple-element.99), channel_id=1, source_target_pairs={{16,0},{32,16},{48,32},{64,48},{80,64},{96,80},{112,96},{128,112},... | collective-permute-start | bytes 152 | tf_op jit(solution)/shard_map/ppermute | solution.py:22
  24.4 6.0 %collective-permute-start.2 = (s32[1,2,12]{2,1,0:T(2,128)S(1)}, s32[1,2,12]{2,1,0:T(2,128)S(1)}, u32[]{:S(2)}, u32[]{:S(2)}) collective-permute-start(s32[1,2,12]{2,1,0:T(2,128)S(1)} %get-tuple-element.96), channel_id=1, source_target_pairs={{0,16},{16,32},{32,48},{48,64},{64,80},{80,96},{96,112},{112,128},... | collective-permute-start | bytes 296 | tf_op jit(solution)/shard_map/ppermute | solution.py:19
  28.5 4.9 %collective-permute-start.3 = (s32[1,2,12]{2,1,0:T(2,128)S(1)}, s32[1,2,12]{2,1,0:T(2,128)S(1)}, u32[]{:S(2)}, u32[]{:S(2)}) collective-permute-start(s32[1,2,12]{2,1,0:T(2,128)S(1)} %get-tuple-element.97), channel_id=1, source_target_pairs={{16,0},{32,16},{48,32},{64,48},{80,64},{96,80},{112,96},{128,112},... | collective-permute-start | bytes 296 | tf_op jit(solution)/shard_map/ppermute | solution.py:22
  37.1 5.5 %collective-permute-start.6 = (f32[1,2,2,32,512]{4,3,1,0,2:T(8,128)S(1)}, f32[1,2,2,32,512]{4,3,1,0,2:T(8,128)S(1)}, u32[]{:S(2)}, u32[]{:S(2)}) collective-permute-start(f32[1,2,2,32,512]{4,3,1,0,2:T(8,128)S(1)} %copy.113), channel_id=1, source_target_pairs={{0,16},{16,32},{32,48},{48,64},{64,80},{80,96},{96,112},{112,128},... | collective-permute-start | bytes 786440 | tf_op jit(solution)/shard_map/ppermute | solution.py:19
  39.1 7.7 %collective-permute-start.7 = (f32[1,2,2,32,512]{4,3,1,0,2:T(8,128)S(1)}, f32[1,2,2,32,512]{4,3,1,0,2:T(8,128)S(1)}, u32[]{:S(2)}, u32[]{:S(2)}) collective-permute-start(f32[1,2,2,32,512]{4,3,1,0,2:T(8,128)S(1)} %copy.115), channel_id=1, source_target_pairs={{16,0},{32,16},{48,32},{64,48},{80,64},{96,80},{112,96},{128,112},... | collective-permute-start | bytes 786440 | tf_op jit(solution)/shard_map/ppermute | solution.py:22
  42.4 4.5 %copy-start.3 = (bf16[512,512]{1,0:T(8,128)(2,1)S(1)}, bf16[512,512]{1,0:T(8,128)(2,1)}, u32[]{:S(2)}) copy-start(bf16[512,512]{1,0:T(8,128)(2,1)} %copy-done.2) | copy-start | bytes 1572868
  42.4 4.5 %copy-start.6 = (bf16[512,512]{1,0:T(8,128)(2,1)S(1)}, bf16[512,512]{1,0:T(8,128)(2,1)}, u32[]{:S(2)}) copy-start(bf16[512,512]{1,0:T(8,128)(2,1)} %copy-done.5) | copy-start | bytes 1572868
  42.4 4.5 %copy-start.9 = (bf16[512,512]{1,0:T(8,128)(2,1)S(1)}, bf16[512,512]{1,0:T(8,128)(2,1)}, u32[]{:S(2)}) copy-start(bf16[512,512]{1,0:T(8,128)(2,1)} %copy-done.8) | copy-start | bytes 1572868
  46.9 0.9 copy-start.11
  47.9 7.4 %copy-start.15 = (f32[3,2048]{1,0:T(4,128)S(1)}, f32[3,2048]{1,0:T(4,128)}, u32[]{:S(2)}) copy-start(f32[3,2048]{1,0:T(4,128)} %param.24) | copy-start | bytes 73732
  48.5 8.2 %collective-permute-start.9 = (bf16[2,2,2,32,512]{4,3,1,0,2:T(8,128)(2,1)S(1)}, bf16[2,2,2,32,512]{4,3,1,0,2:T(8,128)(2,1)S(1)}, u32[]{:S(2)}, u32[]{:S(2)}) collective-permute-start(bf16[2,2,2,32,512]{4,3,1,0,2:T(8,128)(2,1)S(1)} %pad_maximum_fusion.3), channel_id=1, source_target_pairs={{1,0},{2,1},{3,2},{4,3},{5,4},{6,5},{7,6},{8,7},{9,8},{10,9},{11,1... | collective-permute-start | bytes 786440 | tf_op jit(solution)/shard_map/ppermute | solution.py:22
  53.4 8.3 %collective-permute-start.8 = (bf16[2,2,2,32,512]{4,3,1,0,2:T(8,128)(2,1)S(1)}, bf16[2,2,2,32,512]{4,3,1,0,2:T(8,128)(2,1)S(1)}, u32[]{:S(2)}, u32[]{:S(2)}) collective-permute-start(bf16[2,2,2,32,512]{4,3,1,0,2:T(8,128)(2,1)S(1)} %pad_maximum_fusion.3), channel_id=1, source_target_pairs={{0,1},{1,2},{2,3},{3,4},{4,5},{5,6},{6,7},{7,8},{8,9},{9,10},{10,1... | collective-permute-start | bytes 786440 | tf_op jit(solution)/shard_map/ppermute | solution.py:19
  65.0 8.8 %collective-permute-start.10 = (f32[1,2,2,32,512]{4,3,1,0,2:T(8,128)S(1)}, f32[1,2,2,32,512]{4,3,1,0,2:T(8,128)S(1)}, u32[]{:S(2)}, u32[]{:S(2)}) collective-permute-start(f32[1,2,2,32,512]{4,3,1,0,2:T(8,128)S(1)} %copy.119), channel_id=1, source_target_pairs={{0,16},{16,32},{32,48},{48,64},{64,80},{80,96},{96,112},{112,128},... | collective-permute-start | bytes 786440 | tf_op jit(solution)/shard_map/ppermute | solution.py:19
  70.5 7.7 %collective-permute-start.11 = (f32[1,2,2,32,512]{4,3,1,0,2:T(8,128)S(1)}, f32[1,2,2,32,512]{4,3,1,0,2:T(8,128)S(1)}, u32[]{:S(2)}, u32[]{:S(2)}) collective-permute-start(f32[1,2,2,32,512]{4,3,1,0,2:T(8,128)S(1)} %copy.121), channel_id=1, source_target_pairs={{16,0},{32,16},{48,32},{64,48},{80,64},{96,80},{112,96},{128,112},... | collective-permute-start | bytes 786440 | tf_op jit(solution)/shard_map/ppermute | solution.py:22
  73.4 5.0 %copy-start.4 = (bf16[512,512]{1,0:T(8,128)(2,1)S(1)}, bf16[512,512]{1,0:T(8,128)(2,1)}, u32[]{:S(2)}) copy-start(bf16[512,512]{1,0:T(8,128)(2,1)} %copy-done.2) | copy-start | bytes 1572868
  73.4 5.0 %copy-start.7 = (bf16[512,512]{1,0:T(8,128)(2,1)S(1)}, bf16[512,512]{1,0:T(8,128)(2,1)}, u32[]{:S(2)}) copy-start(bf16[512,512]{1,0:T(8,128)(2,1)} %copy-done.5) | copy-start | bytes 1572868
  73.4 5.0 %copy-start.10 = (bf16[512,512]{1,0:T(8,128)(2,1)S(1)}, bf16[512,512]{1,0:T(8,128)(2,1)}, u32[]{:S(2)}) copy-start(bf16[512,512]{1,0:T(8,128)(2,1)} %copy-done.8) | copy-start | bytes 1572868
  104.1 23.9 %all-to-all-start.1 = ((bf16[32,2,2,2048]{3,2,1,0:T(2,128)(2,1)}), bf16[32,2,2,2048]{3,2,1,0:T(2,128)(2,1)S(1)}, u32[]{:S(2)}, u32[]{:S(2)}) async-start(bf16[32,2,2,2048]{3,2,1,0:T(2,128)(2,1)} %broadcast_in_dim.47), calls=%async_computation.1 | async-start | bytes 1048576 | tf_op jit(solution)/shard_map/all_to_all | solution.py:41
where the time goes:
time: 148 us; the launch traced here: 147 us
  starting transfers between devices  56.4 us (38%)
  waiting for transfers between devices  27.9 us (19%)
  matrix products  25 us (17%)
  blocking collectives  21.1 us (14%)
  local copies, waits for them, and re-layouts  11.2 us (8%)
  other arithmetic  3.96 us (3%)
  between operations  1.48 us (1%)
    ppermute x6, starting transfers between devices, padded(): lax.ppermute(lax.slice_in_dim(block, 0, width, axis=dim), axis, backward)  24.9 us
    all_to_all x1, blocking collectives, sum_at_owner(): lax.all_to_all(blocks, axis, split_axis=0, concat_axis=0, tiled=True)  21.1 us
    ppermute x6, starting transfers between devices, padded(): lax.ppermute(lax.slice_in_dim(block, block.shape[dim] - width, None, axis...  18.9 us
    all_to_all x1, starting transfers between devices, copy_for_each(): return lax.all_to_all(copies, axis, split_axis=0, concat_axis=0, tiled=True)  12.6 us
    ppermute x6, waiting for transfers between devices, padded(): lax.ppermute(lax.slice_in_dim(block, 0, width, axis=dim), axis, backward)  12.1 us
    all_to_all x1, waiting for transfers between devices, copy_for_each(): return lax.all_to_all(copies, axis, split_axis=0, concat_axis=0, tiled=True)  10.5 us
    ppermute x6, waiting for transfers between devices, padded(): lax.ppermute(lax.slice_in_dim(block, block.shape[dim] - width, None, axis...  5.31 us
    dot_general x1, matrix products, local(): jnp.dot(owned_far[1], sin_table, precision=high)  5.07 us
  transfers between devices with their start and end apart: 13, of which 7 were waited for; matrix products, arithmetic and copies ran while one was open for 3% of the time, Pallas kernels for 0%

commit v1 on v0

v1 whole, which is shorter than its diff:
```python
import math

import numpy as np

import jax
import jax.numpy as jnp
from jax import lax
from jax.experimental import pallas as pl
from jax.experimental.pallas import tpu as pltpu
from jax.sharding import PartitionSpec as P

MESH = pl.DeviceIdType.MESH
F32 = jnp.float32
BF16 = jnp.bfloat16
SLOTS = 12
G = 4
KC = 8
TW = 16
LN = 128


def fft(values):
    size = len(values)
    if size == 1:
        return values
    even = fft(values[0::2])
    odd = fft(values[1::2])
    low, high = [], []
    for t in range(size // 2):
        re, im = odd[t]
        if t == 0:
            pass
        elif 4 * t == size:
            re, im = im, -re
        else:
            c = math.cos(2 * math.pi * t / size)
            s = math.sin(2 * math.pi * t / size)
            if 8 * t == size:
                re, im = (re + im) * c, (im - re) * c
            elif 8 * t == 3 * size:
                re, im = (im - re) * s, (re + im) * (-s)
            else:
                re, im = re * c + im * s, im * c - re * s
        er, ei = even[t]
        low.append((er + re, ei + im))
        high.append((er - re, ei - im))
    return low + high


def doubling(count):
    radii, radius = [], 1
    while 2 * radius <= count // 2:
        radii.append(radius)
        radius *= 2
    return radii


def make_kernel(n_px, n_z, illum, rcv):
    cols_total = 2 * n_z
    patches = 4 * n_px * n_z
    qp = LN // n_px
    rows_p = 2 * qp
    kz = illum // n_z
    hz = KC // kz
    z_rounds = doubling(n_z)
    x_rounds = doubling(n_px)
    scale = 0.125 / (patches * rcv)

    def kernel(
        cin_h, rad_h, far_h, refl_h, cen_h, sd_h, rd_h, part_h, cnt_h, pw_h, fm_h, tw_h,
        cur_h, img_o,
        cin_v, rad_v, radt_v, far_v, refl_v, cen_v, sd_v, rd_v, part_v, cnt_v, pw_v, fm_v, tw_v,
        w_v, wr_v, cs_v, cv_v, cinc_v, x_v, own_v, zr_v, acc_v, push_v, pr_v, curf_v,
        u_v, y_v, sb_v, rb_v, zs_v, zb_v, cur_v,
        in_sem, w_sem, zx_sem, px_sem, rs_sem, zs_sem, out_sem, zd_sem, xd_sem,
    ):
        pi = lax.axis_index("px")
        zi = lax.axis_index("py")

        def ring(value, count):
            return lax.rem(value + count, count)

        z_nb = (ring(zi - 1, n_z), ring(zi + 1, n_z))
        x_nb = (ring(pi - 1, n_px), ring(pi + 1, n_px))

        def z_dev(z):
            return (pi, z)

        def x_dev(x):
            return (x, zi)

        barrier = pltpu.get_barrier_semaphore()
        for z in z_nb:
            pl.semaphore_signal(barrier, inc=1, device_id=z_dev(z), device_id_type=MESH)
        for x in x_nb:
            pl.semaphore_signal(barrier, inc=1, device_id=x_dev(x), device_id_type=MESH)

        ins = []
        for n, (src, dst) in enumerate(
            (
                (cin_h, cin_v), (sd_h, sd_v), (cen_h, cen_v), (rad_h, rad_v),
                (part_h, part_v), (cnt_h, cnt_v), (pw_h, pw_v), (refl_h, refl_v),
                (rd_h, rd_v), (tw_h, tw_v), (fm_h, fm_v), (far_h, far_v),
            )
        ):
            copy = pltpu.make_async_copy(src, dst, in_sem.at[n])
            copy.start()
            ins.append(copy)
        (i_cin, i_sd, i_cen, i_rad, i_part, i_cnt, i_pw, i_refl, i_rd, i_tw, i_fm, i_far) = ins

        def phases(dirs, out):
            for a in range(2):
                for b in range(2):
                    total = None
                    for d in range(3):
                        term = dirs[d : d + 1, :] * cen_v[d, a : a + 1, b : b + 1]
                        total = term if total is None else total + term
                    out[0, 2 * a + b : 2 * a + b + 1, :] = total
            phi = out[0, 0:4, :]
            out[0, 0:4, :] = jnp.cos(phi)
            out[1, 0:4, :] = jnp.sin(phi)

        i_sd.wait()
        i_cen.wait()
        phases(sd_v, cs_v)

        i_cin.wait()
        for p in range(4):
            x0 = cin_v[p // 2, p % 2, 0].astype(F32)
            x1 = cin_v[p // 2, p % 2, 1].astype(F32)
            for g in range(G):
                both = jnp.concatenate([x0[KC * g : KC * g + KC], x1[KC * g : KC * g + KC]], axis=0)
                cinc_v[g, 16 * p : 16 * p + 16, :] = both.astype(BF16)
        i_rad.wait()

        def spectrum(x):
            x0 = jnp.dot(x, rad_v[0], preferred_element_type=F32)
            x1 = jnp.dot(x, rad_v[1], preferred_element_type=F32)
            out = []
            for p in range(4):
                r, i = 16 * p, 16 * p + 8
                out.append((x0[r : r + 8] - x1[i : i + 8], x1[r : r + 8] + x0[i : i + 8]))
            return out

        def z_copy(t, g, d):
            return pltpu.make_async_remote_copy(
                src_ref=own_v.at[t, g],
                dst_ref=zr_v.at[t, g, 1 - d],
                send_sem=zx_sem.at[0, t, g, d],
                recv_sem=zx_sem.at[1, t, g, 1 - d],
                device_id=z_dev(z_nb[d]),
                device_id_type=MESH,
            )

        def x_copy(t, g, d):
            return pltpu.make_async_remote_copy(
                src_ref=push_v.at[t, g, d],
                dst_ref=pr_v.at[t, g, 1 - d],
                send_sem=px_sem.at[0, t, g, d],
                recv_sem=px_sem.at[1, t, g, 1 - d],
                device_id=x_dev(x_nb[d]),
                device_id_type=MESH,
            )

        def w_copy(d):
            return pltpu.make_async_remote_copy(
                src_ref=w_v.at[pl.ds(32 * d, 32)],
                dst_ref=wr_v.at[1 - d],
                send_sem=w_sem.at[0, d],
                recv_sem=w_sem.at[1, 1 - d],
                device_id=x_dev(x_nb[d]),
                device_id_type=MESH,
            )

        def radiate(t, g, x):
            for p, (re, im) in enumerate(spectrum(x)):
                c = cs_v[0, p : p + 1, :]
                s = cs_v[1, p : p + 1, :]
                both = jnp.concatenate([re * c + im * s, im * c - re * s], axis=0)
                own_v[t, g, 16 * p : 16 * p + 16, :] = both.astype(BF16)
            for d in range(2):
                z_copy(t, g, d).start()

        def partner_sums(t, g):
            for d in range(2):
                z_copy(t, g, d).wait_recv()
            for j in range(4):
                lanes = slice(128 * j, 128 * j + 128)

                def source(row, e):
                    if e < 2:
                        return zr_v[t, g, 0, 16 * (2 * row + e) : 16 * (2 * row + e) + 16, lanes]
                    if e < 4:
                        return own_v[t, g, 16 * (2 * row + e - 2) : 16 * (2 * row + e - 2) + 16, lanes]
                    return zr_v[t, g, 1, 16 * (2 * row + e - 4) : 16 * (2 * row + e - 4) + 16, lanes]

                src = [[source(row, e).astype(F32) for e in range(6)] for row in range(2)]
                for a in range(2):
                    for b in range(2):
                        p = 2 * a + b
                        total = None
                        for row in range(2):
                            for dc in range(5):
                                if row == a and dc == 2:
                                    continue
                                o = (row - a + 1) * 5 + dc
                                w = w_v[16 * p + o : 16 * p + o + 1, :]
                                term = w * src[row][b + dc]
                                total = term if total is None else total + term
                        acc_v[g, 16 * p : 16 * p + 16, lanes] = total
                for d in range(2):
                    row = d
                    for b in range(2):
                        total = None
                        for dc in range(5):
                            o = (10 if d == 0 else 0) + dc
                            w = wr_v[d, 16 * b + o : 16 * b + o + 1, :]
                            term = w * src[row][b + dc]
                            total = term if total is None else total + term
                        push_v[t, g, d, 16 * b : 16 * b + 16, lanes] = total.astype(BF16)
            for d in range(2):
                x_copy(t, g, d).start()

        def receive(t, g):
            for d in range(2):
                x_copy(t, g, d).wait_recv()
            for p in range(4):
                a, b = p // 2, p % 2
                total = acc_v[g, 16 * p : 16 * p + 16, :]
                total = total + pr_v[t, g, a, 16 * b : 16 * b + 16, :].astype(F32)
                re, im = total[0:8], total[8:16]
                c = cs_v[0, p : p + 1, :]
                s = cs_v[1, p : p + 1, :]
                both = jnp.concatenate([re * c - im * s, re * s + im * c], axis=0)
                x_v[16 * p : 16 * p + 16, :] = both.astype(BF16)
            x = x_v[...]
            q0 = jnp.dot(x, radt_v[0], preferred_element_type=F32)
            q1 = jnp.dot(x, radt_v[1], preferred_element_type=F32)
            for p in range(4):
                r, i = 16 * p, 16 * p + 8
                got = jnp.concatenate(
                    [q0[r : r + 8] - q1[i : i + 8], q1[r : r + 8] + q0[i : i + 8]], axis=0
                )
                f = refl_v[p // 2, p % 2 : p % 2 + 1, :]
                new = cinc_v[g, 16 * p : 16 * p + 16, :].astype(F32) + f * got
                curf_v[g, 16 * p : 16 * p + 16, :] = new.astype(BF16)
            return curf_v[g]

        def rs_copy(g, d, peer):
            return pltpu.make_async_remote_copy(
                src_ref=sb_v.at[g, peer],
                dst_ref=rb_v.at[g, d],
                send_sem=rs_sem.at[0, g],
                recv_sem=rs_sem.at[1, g],
                device_id=x_dev(peer),
                device_id_type=MESH,
            )

        def rs_all(g):
            return pltpu.make_async_remote_copy(
                src_ref=sb_v.at[g, pl.ds(0, n_px - 1)],
                dst_ref=rb_v.at[g, pl.ds(1, n_px - 1)],
                send_sem=rs_sem.at[0, g],
                recv_sem=rs_sem.at[1, g],
                device_id=x_dev(x_nb[0]),
                device_id_type=MESH,
            )

        def far_field(g):
            for p, (re, im) in enumerate(spectrum(curf_v[g])):
                both = jnp.concatenate([re, im], axis=0)
                x_v[16 * p : 16 * p + 16, :] = both.astype(BF16)
            x = x_v[...]
            for n in range(4):
                beams = jnp.dot(x, far_v[:, 512 * n : 512 * n + 512], preferred_element_type=F32)
                for m in range(4):
                    u = 4 * n + m
                    at = slice(LN * m, LN * m + LN)
                    far_re = far_im = None
                    for p in range(4):
                        br = beams[16 * p : 16 * p + 8, at]
                        bi = beams[16 * p + 8 : 16 * p + 16, at]
                        c = cv_v[0, p : p + 1, LN * u : LN * u + LN]
                        s = cv_v[1, p : p + 1, LN * u : LN * u + LN]
                        tr = br * c - bi * s
                        ti = br * s + bi * c
                        far_re = tr if far_re is None else far_re + tr
                        far_im = ti if far_im is None else far_im + ti
                    u_v[0, u] = far_re
                    u_v[1, u] = far_im
            spec = fft([(u_v[0, u], u_v[1, u]) for u in range(TW)])
            for t in range(0, TW, 2):
                parts = []
                for tt in (t, t + 1):
                    re, im = spec[tt]
                    if tt:
                        c = tw_v[0, tt : tt + 1, :]
                        s = tw_v[1, tt : tt + 1, :]
                        re, im = re * c + im * s, im * c - re * s
                    parts.append((re, im))
                for part in range(2):
                    y_v[8 * t : 8 * t + 16, LN * part : LN * part + LN] = jnp.concatenate(
                        [parts[0][part], parts[1][part]], axis=0
                    ).astype(BF16)
            bins = lax.dot_general(
                fm_v[...], y_v[...], (((1,), (1,)), ((), ())), preferred_element_type=F32
            )
            sb_v[g] = bins.reshape(n_px, rows_p, LN).astype(BF16)

            def send(d, carry):
                rs_copy(g, d, ring(pi + d, n_px)).start()
                return carry

            lax.fori_loop(1, n_px, send, 0)

        def z_sum_copy(g, owner):
            return pltpu.make_async_remote_copy(
                src_ref=zs_v.at[g],
                dst_ref=zb_v.at[ring(zi - owner, n_z)],
                send_sem=zs_sem.at[0],
                recv_sem=zs_sem.at[1],
                device_id=z_dev(owner),
                device_id_type=MESH,
            )

        def gather_bins(g):
            rs_all(g).wait_recv()
            total = sb_v[g, pi].astype(F32)
            for d in range(1, n_px):
                total = total + rb_v[g, d].astype(F32)
            zs_v[g] = total.astype(BF16)
            for h in range(hz):
                owner = hz * g + h

                @pl.when(zi != owner)
                def _():
                    z_sum_copy(g, owner).start()

        i_part.wait()
        i_cnt.wait()
        i_pw.wait()
        for a in range(2):
            for b in range(2):
                ids = part_v[a, b : b + 1, :]
                row = ids // cols_total
                col = ids - row * cols_total
                dr = row - (2 * pi + a) + 1
                dc = (col - (2 * zi + b) + 2 + cols_total) % cols_total
                slot = lax.broadcasted_iota(jnp.int32, (1, SLOTS), 1)
                live = slot < cnt_v[a : a + 1, b : b + 1]
                w = jnp.where(live, pw_v[a, b : b + 1, :].astype(F32), 0.0)
                kind = dr * 5 + dc
                offsets = lax.broadcasted_iota(jnp.int32, (16, SLOTS), 0)
                table = jnp.where(offsets == kind, jnp.broadcast_to(w, (16, SLOTS)), 0.0)
                column = jnp.sum(table, axis=1, keepdims=True)
                p = 2 * a + b
                w_v[16 * p : 16 * p + 16, :] = jnp.broadcast_to(column, (16, LN))

        pl.semaphore_wait(barrier, 4)
        for d in range(2):
            w_copy(d).start()
        for g in range(G):
            radiate(0, g, cinc_v[g])

        rounds = (
            (zd_sem, z_rounds, z_dev, zi, n_z),
            (xd_sem, x_rounds, x_dev, pi, n_px),
        )

        def tell(n):
            for sem, radii, dev, me, count in rounds:
                if n < len(radii):
                    for side in (-radii[n], radii[n]):
                        pl.semaphore_signal(
                            sem.at[n],
                            inc=1,
                            device_id=dev(ring(me + side, count)),
                            device_id_type=MESH,
                        )

        def hear(n):
            for sem, radii, *_ in rounds:
                if n < len(radii):
                    pl.semaphore_wait(sem.at[n], 2)

        tell(0)

        for part in range(2):
            radt_v[part] = rad_v[part].T
        i_refl.wait()
        i_rd.wait()
        phases(rd_v, cv_v)
        i_tw.wait()
        i_fm.wait()
        i_far.wait()
        for d in range(2):
            w_copy(d).wait_recv()

        partner_sums(0, 0)
        for g in range(G):
            if g + 1 < G:
                partner_sums(0, g + 1)
            radiate(1, g, receive(0, g))
            hear(g)
            tell(g + 1)
        partner_sums(1, 0)
        for g in range(G):
            if g + 1 < G:
                partner_sums(1, g + 1)
            receive(1, g)
            far_field(g)
        for p in range(4):
            for part in range(2):
                whole = jnp.concatenate(
                    [
                        curf_v[g, 16 * p : 16 * p + 16, :].astype(F32)[8 * part : 8 * part + 8]
                        for g in range(G)
                    ],
                    axis=0,
                )
                cur_v[p // 2, p % 2, part] = whole.astype(BF16)
        out = pltpu.make_async_copy(cur_v, cur_h, out_sem)
        out.start()
        for g in range(G):
            gather_bins(g)

        for t in range(2):
            for g in range(G):
                for d in range(2):
                    z_copy(t, g, d).wait_send()
                    x_copy(t, g, d).wait_send()
        for d in range(2):
            w_copy(d).wait_send()
        for g in range(G):
            rs_all(g).wait_send()

        all_z = pltpu.make_async_remote_copy(
            src_ref=zb_v.at[pl.ds(1, n_z - 1)],
            dst_ref=zb_v.at[pl.ds(1, n_z - 1)],
            send_sem=zs_sem.at[0],
            recv_sem=zs_sem.at[1],
            device_id=z_dev(z_nb[0]),
            device_id_type=MESH,
        )
        all_z.wait_recv()
        total = zs_v[zi // hz].astype(F32)
        for d in range(1, n_z):
            total = total + zb_v[d].astype(F32)
        power = total * total
        power = (power[0:qp] + power[qp : 2 * qp]) * scale
        if qp < 8:
            power = jnp.concatenate([power, jnp.zeros((8 - qp, LN), F32)], axis=0)
        width = TW * qp
        lane = lax.broadcasted_iota(jnp.int32, (LN, width), 0)
        bin_id = lax.broadcasted_iota(jnp.int32, (LN, width), 1)
        row_id = lax.broadcasted_iota(jnp.int32, (max(qp, 8), width), 0)
        bin_row = lax.broadcasted_iota(jnp.int32, (max(qp, 8), width), 1) // TW
        first = lax.rem(zi, hz) * kz
        for b in range(kz):
            pick = jnp.where(lane == (bin_id % TW) * KC + first + b, 1.0, 0.0)
            rows = jnp.dot(power, pick, precision=lax.Precision.HIGHEST, preferred_element_type=F32)
            img_o[b : b + 1, :] = jnp.sum(
                jnp.where(row_id == bin_row, rows, 0.0), axis=0, keepdims=True
            )
        all_z.wait_send()
        out.wait()

    return kernel


def tables(n_px):
    qp = LN // n_px
    row = np.arange(2 * LN)
    part_out = (row // qp) % 2
    q = (row // (2 * qp)) * qp + row % qp
    col = np.arange(2 * LN)
    part_in, v = col // LN, col % LN
    turn = (q[:, None] * v[None, :] + (LN // 4) * (part_out[:, None] - part_in[None, :])) % LN
    second = np.cos(2 * math.pi * turn / LN).astype(np.float32)
    angle = 2 * math.pi * np.arange(TW)[:, None] * np.arange(LN)[None, :] / (TW * LN)
    twiddle = np.stack([np.cos(angle), np.sin(angle)]).astype(np.float32)
    return second, twiddle


def solution(mesh):
    n_px, n_z = mesh.shape["px"], mesh.shape["py"]

    def local(cin, rad, far, refl, cen, sd, rd, part, cnt, pw):
        illum, units = cin.shape[3], cin.shape[4]
        rcv = rd.shape[1]
        dirs = sd.shape[1]
        second, twiddle = tables(n_px)
        qp = LN // n_px
        kz = illum // n_z
        kernel = make_kernel(n_px, n_z, illum, rcv)
        V = pltpu.VMEM
        dma = pltpu.SemaphoreType.DMA
        regular = pltpu.SemaphoreType.REGULAR
        scratch = [
            V(cin.shape, BF16),
            V(rad.shape, BF16),
            V((2, dirs, units), BF16),
            V(far.shape, BF16),
            V(refl.shape, F32),
            V(cen.shape, F32),
            V(sd.shape, F32),
            V(rd.shape, F32),
            V(part.shape, jnp.int32),
            V(cnt.shape, jnp.int32),
            V(pw.shape, BF16),
            V((2 * LN, 2 * LN), BF16),
            V((2, TW, LN), F32),
            V((64, LN), F32),
            V((2, 32, LN), F32),
            V((2, 8, dirs), F32),
            V((2, 8, rcv), F32),
            V((G, 64, units), BF16),
            V((64, units), BF16),
            V((2, G, 64, dirs), BF16),
            V((2, G, 2, 64, dirs), BF16),
            V((G, 64, dirs), F32),
            V((2, G, 2, 32, dirs), BF16),
            V((2, G, 2, 32, dirs), BF16),
            V((G, 64, units), BF16),
            V((2, TW, KC, LN), F32),
            V((LN, 2 * LN), BF16),
            V((G, n_px, 2 * qp, LN), BF16),
            V((G, n_px, 2 * qp, LN), BF16),
            V((G, 2 * qp, LN), BF16),
            V((n_z, 2 * qp, LN), BF16),
            V(cin.shape, BF16),
            dma((12,)),
            dma((2, 2)),
            dma((2, 2, G, 2)),
            dma((2, 2, G, 2)),
            dma((2, G)),
            dma((2,)),
            dma,
            regular((max(1, len(doubling(n_z))),)),
            regular((max(1, len(doubling(n_px))),)),
        ]
        return pl.pallas_call(
            kernel,
            out_shape=(
                jax.ShapeDtypeStruct(cin.shape, BF16),
                jax.ShapeDtypeStruct((kz, TW * qp), F32),
            ),
            in_specs=[pl.BlockSpec(memory_space=pl.ANY)] * 12,
            out_specs=(
                pl.BlockSpec(memory_space=pl.ANY),
                pl.BlockSpec(memory_space=pltpu.VMEM),
            ),
            scratch_shapes=scratch,
            compiler_params=pltpu.CompilerParams(
                collective_id=0, has_side_effects=True, vmem_limit_bytes=48 << 20
            ),
        )(
            cin, rad, far, refl, cen, sd, rd, part, cnt, pw,
            jnp.asarray(second, BF16), jnp.asarray(twiddle),
        )

    in_specs = (
        P("px", "py", None, None, None),
        P(),
        P(),
        P("px", "py", None),
        P(None, "px", "py"),
        P(),
        P(),
        P("px", "py", None),
        P("px", "py"),
        P("px", "py", None),
    )
    out_specs = (P("px", "py", None, None, None), P("py", "px"))
    return jax.shard_map(local, mesh=mesh, in_specs=in_specs, out_specs=out_specs, check_vma=False)
```

time: 148 us -> 63.7 us (0.43)
  the two profiles are of different devices: /device:TPU:1 before, /device:TPU:32 now
where the time goes in v1:
time: 63.7 us; the launch traced here: 63.2 us
  Pallas kernels  50.9 us (80%)
  local copies, waits for them, and re-layouts  11.6 us (18%)
  between operations  0.65 us (1%)
    pallas_call x1, Pallas kernels, local(): pl.pallas_call(kernel, out_shape=(jax.ShapeDtypeStruct(cin.shape, BF16),...  50.9 us
    unnamed x25, local copies, waits for them, and re-layouts  11.6 us

profile of v1, /device:TPU:32, one launch (start us, length us, event | category | flops | bytes accessed | tf_op | source)
XLA Modules:
  0.0 63.2 jit_solution(16429914732443285846)
XLA Ops:
  0.6 0.8 %copy.14.cen_h = f32[3,2,2]{2,1,0:T(2,128)S(1)} copy(f32[3,2,2]{0,2,1:T(2,128)} %param.16) | data formatting | bytes 96 | tf_op args[4]
  1.4 0.0 copy-start
  1.4 1.6 %copy-done = bf16[512,2048]{1,0:T(8,128)(2,1)S(1)} copy-done((bf16[512,2048]{1,0:T(8,128)(2,1)S(1)}, bf16[512,2048]{1,0:T(8,128)(2,1)}, u32[]{:S(2)}) %copy-start) | copy-done | bytes 2097176
  3.0 0.0 copy-start.1
  3.0 1.2 %copy-done.1 = bf16[2,512,512]{2,1,0:T(8,128)(2,1)S(1)} copy-done((bf16[2,512,512]{2,1,0:T(8,128)(2,1)S(1)}, bf16[2,512,512]{2,1,0:T(8,128)(2,1)}, u32[]{:S(2)}) %copy-start.1) | copy-done | bytes 1048600
  4.2 0.0 copy-start.2
  4.2 0.9 %copy-done.2 = bf16[2,2,2,32,512]{4,3,2,1,0:T(8,128)(2,1)S(1)} copy-done((bf16[2,2,2,32,512]{4,3,2,1,0:T(8,128)(2,1)S(1)}, bf16[2,2,2,32,512]{4,3,2,1,0:T(8,128)(2,1)}, u32[]{:S(2)}) %copy-start.2) | copy-done | bytes 262168
  5.2 0.0 copy-start.3
  5.2 0.9 %copy-done.3 = bf16[256,256]{1,0:T(8,128)(2,1)S(1)} copy-done((bf16[256,256]{1,0:T(8,128)(2,1)S(1)}, bf16[256,256]{1,0:T(8,128)(2,1)}, u32[]{:S(2)}) %copy-start.3) | copy-done | bytes 131096
  6.1 0.0 copy-start.4
  6.1 0.8 %copy-done.4 = f32[3,2048]{1,0:T(4,128)S(1)} copy-done((f32[3,2048]{1,0:T(4,128)S(1)}, f32[3,2048]{1,0:T(4,128)}, u32[]{:S(2)}) %copy-start.4) | copy-done | bytes 24600
  6.8 0.0 copy-start.5
  6.8 0.7 %copy-done.5 = f32[2,16,128]{2,1,0:T(8,128)S(1)} copy-done((f32[2,16,128]{2,1,0:T(8,128)S(1)}, f32[2,16,128]{2,1,0:T(8,128)}, u32[]{:S(2)}) %copy-start.5) | copy-done | bytes 16408
  7.6 0.0 copy-start.6
  7.6 0.7 %copy-done.6 = f32[2,2,512]{2,1,0:T(2,128)S(1)} copy-done((f32[2,2,512]{2,1,0:T(2,128)S(1)}, f32[2,2,512]{2,1,0:T(2,128)}, u32[]{:S(2)}) %copy-start.6) | copy-done | bytes 8216
  8.2 0.0 copy-start.7
  8.3 0.7 %copy-done.7 = f32[3,512]{1,0:T(4,128)S(1)} copy-done((f32[3,512]{1,0:T(4,128)S(1)}, f32[3,512]{1,0:T(4,128)}, u32[]{:S(2)}) %copy-start.7) | copy-done | bytes 6168
  8.9 0.0 copy-start.8
  8.9 0.7 %copy-done.8 = s32[2,2,12]{2,1,0:T(2,128)S(1)} copy-done((s32[2,2,12]{2,1,0:T(2,128)S(1)}, s32[2,2,12]{2,1,0:T(2,128)}, u32[]{:S(2)}) %copy-start.8) | copy-done | bytes 216
  9.6 0.0 copy-start.9
  9.6 0.7 %copy-done.9 = s32[2,2]{1,0:T(2,128)S(1)} copy-done((s32[2,2]{1,0:T(2,128)S(1)}, s32[2,2]{1,0:T(2,128)}, u32[]{:S(2)}) %copy-start.9) | copy-done | bytes 40
  10.3 0.0 copy-start.10
  10.3 0.7 %copy-done.10 = bf16[2,2,12]{2,1,0:T(2,128)(2,1)S(1)} copy-done((bf16[2,2,12]{2,1,0:T(2,128)(2,1)S(1)}, bf16[2,2,12]{2,1,0:T(2,128)(2,1)}, u32[]{:S(2)}) %copy-start.10) | copy-done | bytes 120
  11.0 50.9 %shard_map.131 = (bf16[2,2,2,32,512]{4,3,2,1,0:T(8,128)(2,1)S(1)}, f32[2,64]{1,0:T(2,128)S(1)}) custom-call(bf16[2,2,2,32,512]{4,3,2,1,0:T(8,128)(2,1)S(1)} %copy-done.2, bf16[2,512,512]{2,1,0:T(8,128)(2,1)S(1)} %copy-done.1, bf16[512,2048]{1,0:T(8,128)(2,1)S(1)} %copy-done, f32[2,2,512]{2,1,0:T(2,128)S(1)} %copy-done.6, f32[3,2,2]{2,1,0:T(2,128)S(1)} %copy.14.cen_h, ...), custom_call_target="tpu_custom_call" | custom-call | tf_op jit(solution)/shard_map/pallas_call | solution.py:542
  61.9 0.7 %copy.17 = bf16[2,2,2,32,512]{4,3,2,1,0:T(8,128)(2,1)} copy(bf16[2,2,2,32,512]{4,3,2,1,0:T(8,128)(2,1)S(1)} %get-tuple-element.4) | data formatting | bytes 524288
  62.6 0.6 copy.18
Async XLA Ops:
  1.4 1.6 %copy-start = (bf16[512,2048]{1,0:T(8,128)(2,1)S(1)}, bf16[512,2048]{1,0:T(8,128)(2,1)}, u32[]{:S(2)}) copy-start(bf16[512,2048]{1,0:T(8,128)(2,1)} %far_h.1) | copy-start | bytes 6291460
  3.0 1.2 %copy-start.1 = (bf16[2,512,512]{2,1,0:T(8,128)(2,1)S(1)}, bf16[2,512,512]{2,1,0:T(8,128)(2,1)}, u32[]{:S(2)}) copy-start(bf16[2,512,512]{2,1,0:T(8,128)(2,1)} %rad_h.1) | copy-start | bytes 3145732
  4.2 0.9 %copy-start.2 = (bf16[2,2,2,32,512]{4,3,2,1,0:T(8,128)(2,1)S(1)}, bf16[2,2,2,32,512]{4,3,2,1,0:T(8,128)(2,1)}, u32[]{:S(2)}) copy-start(bf16[2,2,2,32,512]{4,3,2,1,0:T(8,128)(2,1)} %cin_h.1) | copy-start | bytes 786436
  5.2 0.9 %copy-start.3 = (bf16[256,256]{1,0:T(8,128)(2,1)S(1)}, bf16[256,256]{1,0:T(8,128)(2,1)}, u32[]{:S(2)}) copy-start(bf16[256,256]{1,0:T(8,128)(2,1)} %constant.4.clone.fm_h) | copy-start | bytes 393220
  6.1 0.8 %copy-start.4 = (f32[3,2048]{1,0:T(4,128)S(1)}, f32[3,2048]{1,0:T(4,128)}, u32[]{:S(2)}) copy-start(f32[3,2048]{1,0:T(4,128)} %rd_h.1) | copy-start | bytes 73732
  6.8 0.7 %copy-start.5 = (f32[2,16,128]{2,1,0:T(8,128)S(1)}, f32[2,16,128]{2,1,0:T(8,128)}, u32[]{:S(2)}) copy-start(f32[2,16,128]{2,1,0:T(8,128)} %constant.5.clone.tw_h) | copy-start | bytes 49156
  7.6 0.7 %copy-start.6 = (f32[2,2,512]{2,1,0:T(2,128)S(1)}, f32[2,2,512]{2,1,0:T(2,128)}, u32[]{:S(2)}) copy-start(f32[2,2,512]{2,1,0:T(2,128)} %refl_h.1) | copy-start | bytes 24580
  8.2 0.7 %copy-start.7 = (f32[3,512]{1,0:T(4,128)S(1)}, f32[3,512]{1,0:T(4,128)}, u32[]{:S(2)}) copy-start(f32[3,512]{1,0:T(4,128)} %sd_h.1) | copy-start | bytes 18436
  8.9 0.7 %copy-start.8 = (s32[2,2,12]{2,1,0:T(2,128)S(1)}, s32[2,2,12]{2,1,0:T(2,128)}, u32[]{:S(2)}) copy-start(s32[2,2,12]{2,1,0:T(2,128)} %part_h.1) | copy-start | bytes 580
  9.6 0.7 %copy-start.9 = (s32[2,2]{1,0:T(2,128)S(1)}, s32[2,2]{1,0:T(2,128)}, u32[]{:S(2)}) copy-start(s32[2,2]{1,0:T(2,128)} %cnt_h.1) | copy-start | bytes 52
  10.3 0.7 %copy-start.10 = (bf16[2,2,12]{2,1,0:T(2,128)(2,1)S(1)}, bf16[2,2,12]{2,1,0:T(2,128)(2,1)}, u32[]{:S(2)}) copy-start(bf16[2,2,12]{2,1,0:T(2,128)(2,1)} %pw_h.1) | copy-start | bytes 292

commit v2 on v1

--- a/solution.py
+++ b/solution.py
@@ -47,9 +47,9 @@
     return low + high
 
 
-def doubling(count):
+def doubling(reach):
     radii, radius = [], 1
-    while 2 * radius <= count // 2:
+    while radius < reach:
         radii.append(radius)
         radius *= 2
     return radii
@@ -62,17 +62,17 @@
     rows_p = 2 * qp
     kz = illum // n_z
     hz = KC // kz
-    z_rounds = doubling(n_z)
-    x_rounds = doubling(n_px)
+    z_rounds = doubling(n_z // 2)
+    x_rounds = doubling(n_px - 1)
     scale = 0.125 / (patches * rcv)
 
     def kernel(
         cin_h, rad_h, far_h, refl_h, cen_h, sd_h, rd_h, part_h, cnt_h, pw_h, fm_h, tw_h,
-        cur_h, img_o,
+        cur_o, img_o,
         cin_v, rad_v, radt_v, far_v, refl_v, cen_v, sd_v, rd_v, part_v, cnt_v, pw_v, fm_v, tw_v,
         w_v, wr_v, cs_v, cv_v, cinc_v, x_v, own_v, zr_v, acc_v, push_v, pr_v, curf_v,
-        u_v, y_v, sb_v, rb_v, zs_v, zb_v, cur_v,
-        in_sem, w_sem, zx_sem, px_sem, rs_sem, zs_sem, out_sem, zd_sem, xd_sem,
+        u_v, y_v, sb_v, rb_v, zs_v, zb_v,
+        in_sem, w_sem, zx_sem, px_sem, rs_sem, zs_sem, zd_sem, xd_sem,
     ):
         pi = lax.axis_index("px")
         zi = lax.axis_index("py")
@@ -82,6 +82,7 @@
 
         z_nb = (ring(zi - 1, n_z), ring(zi + 1, n_z))
         x_nb = (ring(pi - 1, n_px), ring(pi + 1, n_px))
+        has_x = (pi > 0, pi < n_px - 1)
 
         def z_dev(z):
             return (pi, z)
@@ -92,33 +93,46 @@
         barrier = pltpu.get_barrier_semaphore()
         for z in z_nb:
             pl.semaphore_signal(barrier, inc=1, device_id=z_dev(z), device_id_type=MESH)
-        for x in x_nb:
-            pl.semaphore_signal(barrier, inc=1, device_id=x_dev(x), device_id_type=MESH)
+        for d in range(2):
+
+            @pl.when(has_x[d])
+            def _():
+                pl.semaphore_signal(barrier, inc=1, device_id=x_dev(x_nb[d]), device_id_type=MESH)
+
 
         ins = []
         for n, (src, dst) in enumerate(
             (
-                (cin_h, cin_v), (sd_h, sd_v), (cen_h, cen_v), (rad_h, rad_v),
-                (part_h, part_v), (cnt_h, cnt_v), (pw_h, pw_v), (refl_h, refl_v),
+                (sd_h, sd_v), (cen_h, cen_v), (part_h, part_v), (cnt_h, cnt_v),
+                (pw_h, pw_v), (cin_h, cin_v), (rad_h, rad_v), (refl_h, refl_v),
                 (rd_h, rd_v), (tw_h, tw_v), (fm_h, fm_v), (far_h, far_v),
             )
         ):
             copy = pltpu.make_async_copy(src, dst, in_sem.at[n])
             copy.start()
             ins.append(copy)
-        (i_cin, i_sd, i_cen, i_rad, i_part, i_cnt, i_pw, i_refl, i_rd, i_tw, i_fm, i_far) = ins
+        (i_sd, i_cen, i_part, i_cnt, i_pw, i_cin, i_rad, i_refl, i_rd, i_tw, i_fm, i_far) = ins
 
         def phases(dirs, out):
             for a in range(2):
                 for b in range(2):
                     total = None
                     for d in range(3):
-                        term = dirs[d : d + 1, :] * cen_v[d, a : a + 1, b : b + 1]
+                        term = dirs[d : d + 1, :] * cen_v[a, b : b + 1, d : d + 1]
                         total = term if total is None else total + term
                     out[0, 2 * a + b : 2 * a + b + 1, :] = total
             phi = out[0, 0:4, :]
             out[0, 0:4, :] = jnp.cos(phi)
             out[1, 0:4, :] = jnp.sin(phi)
+
+        for d in range(2):
+
+            @pl.when(jnp.logical_not(has_x[d]))
+            def _():
+                wr_v[d] = jnp.zeros(wr_v.shape[1:], F32)
+                for t in range(2):
+                    for g in range(G):
+                        pr_v[t, g, d] = jnp.zeros(pr_v.shape[3:], BF16)
 
         i_sd.wait()
         i_cen.wait()
@@ -219,11 +233,19 @@
                             total = term if total is None else total + term
                         push_v[t, g, d, 16 * b : 16 * b + 16, lanes] = total.astype(BF16)
             for d in range(2):
-                x_copy(t, g, d).start()
+
+                @pl.when(has_x[d])
+                def _():
+                    x_copy(t, g, d).start()
+
 
         def receive(t, g):
             for d in range(2):
-                x_copy(t, g, d).wait_recv()
+
+                @pl.when(has_x[d])
+                def _():
+                    x_copy(t, g, 1 - d).wait_recv()
+
             for p in range(4):
                 a, b = p // 2, p % 2
                 total = acc_v[g, 16 * p : 16 * p + 16, :]
@@ -262,7 +284,7 @@
                 dst_ref=rb_v.at[g, pl.ds(1, n_px - 1)],
                 send_sem=rs_sem.at[0, g],
                 recv_sem=rs_sem.at[1, g],
-                device_id=x_dev(x_nb[0]),
+                device_id=x_dev(ring(pi + 1, n_px)),
                 device_id_type=MESH,
             )
 
@@ -356,34 +378,46 @@
                 p = 2 * a + b
                 w_v[16 * p : 16 * p + 16, :] = jnp.broadcast_to(column, (16, LN))
 
-        pl.semaphore_wait(barrier, 4)
+        pl.semaphore_wait(barrier, 2 + (pi > 0).astype(jnp.int32) + (pi < n_px - 1).astype(jnp.int32))
         for d in range(2):
-            w_copy(d).start()
+
+            @pl.when(has_x[d])
+            def _():
+                w_copy(d).start()
+
         for g in range(G):
             radiate(0, g, cinc_v[g])
 
-        rounds = (
-            (zd_sem, z_rounds, z_dev, zi, n_z),
-            (xd_sem, x_rounds, x_dev, pi, n_px),
-        )
-
-        def tell(n):
-            for sem, radii, dev, me, count in rounds:
-                if n < len(radii):
-                    for side in (-radii[n], radii[n]):
+        def z_tell(n):
+            if n < len(z_rounds):
+                for side in (-z_rounds[n], z_rounds[n]):
+                    pl.semaphore_signal(
+                        zd_sem.at[n], inc=1, device_id=z_dev(ring(zi + side, n_z)), device_id_type=MESH
+                    )
+
+        def z_hear(n):
+            if n < len(z_rounds):
+                pl.semaphore_wait(zd_sem.at[n], 2)
+
+        def x_tell(n):
+            if n < len(x_rounds):
+                for side in (-x_rounds[n], x_rounds[n]):
+                    other = pi + side
+
+                    @pl.when((other >= 0) & (other < n_px))
+                    def _():
                         pl.semaphore_signal(
-                            sem.at[n],
-                            inc=1,
-                            device_id=dev(ring(me + side, count)),
-                            device_id_type=MESH,
+                            xd_sem.at[n], inc=1, device_id=x_dev(other), device_id_type=MESH
                         )
 
-        def hear(n):
-            for sem, radii, *_ in rounds:
-                if n < len(radii):
-                    pl.semaphore_wait(sem.at[n], 2)
-
-        tell(0)
+        def x_hear(n):
+            if n < len(x_rounds):
+                low = (pi - x_rounds[n] >= 0).astype(jnp.int32)
+                high = (pi + x_rounds[n] < n_px).astype(jnp.int32)
+                pl.semaphore_wait(xd_sem.at[n], low + high)
+
+        z_tell(0)
+        x_tell(0)
 
         for part in range(2):
             radt_v[part] = rad_v[part].T
@@ -394,21 +428,36 @@
         i_fm.wait()
         i_far.wait()
         for d in range(2):
-            w_copy(d).wait_recv()
-
-        partner_sums(0, 0)
+
+            @pl.when(has_x[d])
+            def _():
+                w_copy(1 - d).wait_recv()
+
+        x_hear(0)
+        x_tell(1)
         for g in range(G):
-            if g + 1 < G:
-                partner_sums(0, g + 1)
+            partner_sums(0, g)
+        x_hear(1)
+        x_tell(2)
+        z_hear(0)
+        z_tell(1)
+        for g in range(G):
             radiate(1, g, receive(0, g))
-            hear(g)
-            tell(g + 1)
-        partner_sums(1, 0)
+        x_hear(2)
+        x_tell(3)
+        z_hear(1)
+        z_tell(2)
         for g in range(G):
-            if g + 1 < G:
-                partner_sums(1, g + 1)
+            partner_sums(1, g)
+            if g == 0:
+                x_hear(3)
+                x_tell(4)
+        for g in range(G):
             receive(1, g)
+            if g == 0:
+                x_hear(4)
             far_field(g)
+        z_hear(2)
         for p in range(4):
             for part in range(2):
                 whole = jnp.concatenate(
@@ -418,9 +467,7 @@
                     ],
                     axis=0,
                 )
-                cur_v[p // 2, p % 2, part] = whole.astype(BF16)
-        out = pltpu.make_async_copy(cur_v, cur_h, out_sem)
-        out.start()
+                cur_o[p // 2, p % 2, part] = whole.astype(BF16)
         for g in range(G):
             gather_bins(g)
 
@@ -428,9 +475,15 @@
             for g in range(G):
                 for d in range(2):
                     z_copy(t, g, d).wait_send()
-                    x_copy(t, g, d).wait_send()
         for d in range(2):
-            w_copy(d).wait_send()
+
+            @pl.when(has_x[d])
+            def _():
+                w_copy(d).wait_send()
+                for t in range(2):
+                    for g in range(G):
+                        x_copy(t, g, d).wait_send()
+
         for g in range(G):
             rs_all(g).wait_send()
 
@@ -463,7 +516,6 @@
                 jnp.where(row_id == bin_row, rows, 0.0), axis=0, keepdims=True
             )
         all_z.wait_send()
-        out.wait()
 
     return kernel
 
@@ -502,7 +554,7 @@
             V((2, dirs, units), BF16),
             V(far.shape, BF16),
             V(refl.shape, F32),
-            V(cen.shape, F32),
+            V((2, 2, 3), F32),
             V(sd.shape, F32),
             V(rd.shape, F32),
             V(part.shape, jnp.int32),
@@ -528,34 +580,32 @@
             V((G, n_px, 2 * qp, LN), BF16),
             V((G, 2 * qp, LN), BF16),
             V((n_z, 2 * qp, LN), BF16),
-            V(cin.shape, BF16),
             dma((12,)),
             dma((2, 2)),
             dma((2, 2, G, 2)),
             dma((2, 2, G, 2)),
             dma((2, G)),
             dma((2,)),
-            dma,
-            regular((max(1, len(doubling(n_z))),)),
-            regular((max(1, len(doubling(n_px))),)),
+            regular((max(1, len(doubling(n_z // 2))),)),
+            regular((max(1, len(doubling(n_px - 1))),)),
         ]
         return pl.pallas_call(
             kernel,
             out_shape=(
-                jax.ShapeDtypeStruct(cin.shape, BF16),
-                jax.ShapeDtypeStruct((kz, TW * qp), F32),
+                pltpu.VMEM(cin.shape, BF16),
+                pltpu.VMEM((kz, TW * qp), F32),
             ),
-            in_specs=[pl.BlockSpec(memory_space=pl.ANY)] * 12,
+            in_specs=[pl.BlockSpec(memory_space=pltpu.HBM)] * 12,
             out_specs=(
-                pl.BlockSpec(memory_space=pl.ANY),
+                pl.BlockSpec(memory_space=pltpu.VMEM),
                 pl.BlockSpec(memory_space=pltpu.VMEM),
             ),
             scratch_shapes=scratch,
             compiler_params=pltpu.CompilerParams(
-                collective_id=0, has_side_effects=True, vmem_limit_bytes=48 << 20
+                collective_id=0, has_side_effects=True, vmem_limit_bytes=60 << 20
             ),
         )(
-            cin, rad, far, refl, cen, sd, rd, part, cnt, pw,
+            cin, rad, far, refl, jnp.transpose(cen, (1, 2, 0)), sd, rd, part, cnt, pw,
             jnp.asarray(second, BF16), jnp.asarray(twiddle),
         )
 

time: 63.7 us -> 47 us (0.74)
  the two profiles are of different devices: /device:TPU:32 before, /device:TPU:1 now
where the time goes in v2:
time: 47 us; the launch traced here: 46.9 us
  Pallas kernels  44.9 us (96%)
  local copies, waits for them, and re-layouts  1.27 us (3%)
  between operations  0.64 us (1%)
    pallas_call x1, Pallas kernels, local(): pl.pallas_call(kernel, out_shape=(pltpu.VMEM(cin.shape, BF16), pltpu.VMEM...  44.9 us
    unnamed x2, local copies, waits for them, and re-layouts  1.27 us

profile of v2, /device:TPU:1, one launch (start us, length us, event | category | flops | bytes accessed | tf_op | source)
XLA Modules:
  0.0 46.9 jit_solution(10568182302540129846)
XLA Ops:
  0.6 44.9 %shard_map.131 = (bf16[2,2,2,32,512]{4,3,2,1,0:T(8,128)(2,1)S(1)}, f32[2,64]{1,0:T(2,128)S(1)}) custom-call(bf16[2,2,2,32,512]{4,3,2,1,0:T(8,128)(2,1)} %cin_h.1, bf16[2,512,512]{2,1,0:T(8,128)(2,1)} %rad_h.1, bf16[512,2048]{1,0:T(8,128)(2,1)} %far_h.1, f32[2,2,512]{2,1,0:T(2,128)} %refl_h.1, f32[2,2,3]{2,1,0:T(2,128)} %bitcast.1, f32[3,512]{1,0:T(4,128)} %sd_h.1, ...), custom_call_target="tpu_custom_call" | custom-call | tf_op jit(solution)/shard_map/pallas_call | solution.py:592
  45.6 0.7 %copy.16 = bf16[2,2,2,32,512]{4,3,2,1,0:T(8,128)(2,1)} copy(bf16[2,2,2,32,512]{4,3,2,1,0:T(8,128)(2,1)S(1)} %get-tuple-element.2) | data formatting | bytes 524288
  46.3 0.6 %copy.17 = f32[2,64]{1,0:T(2,128)} copy(f32[2,64]{1,0:T(2,128)S(1)} %get-tuple-element.3) | data formatting | bytes 1024

commit v3 on v2

--- a/solution.py
+++ b/solution.py
@@ -70,9 +70,9 @@
         cin_h, rad_h, far_h, refl_h, cen_h, sd_h, rd_h, part_h, cnt_h, pw_h, fm_h, tw_h,
         cur_o, img_o,
         cin_v, rad_v, radt_v, far_v, refl_v, cen_v, sd_v, rd_v, part_v, cnt_v, pw_v, fm_v, tw_v,
-        w_v, wr_v, cs_v, cv_v, cinc_v, x_v, own_v, zr_v, acc_v, push_v, pr_v, curf_v,
-        u_v, y_v, sb_v, rb_v, zs_v, zb_v,
-        in_sem, w_sem, zx_sem, px_sem, rs_sem, zs_sem, zd_sem, xd_sem,
+        w_v, wr_v, nrefl_v, ncen_v, cs_v, cv_v, cinc_v, x_v, own_v, zr_v, acc_v, push_v, pr_v, curf_v,
+        u_v, xf_v, y_v, sb_v, rb_v, zs_v, zb_v,
+        in_sem, w_sem, n_sem, zx_sem, px_sem, rs_sem, zs_sem, zd_sem, xd_sem,
     ):
         pi = lax.axis_index("px")
         zi = lax.axis_index("py")
@@ -109,34 +109,36 @@
             )
         ):
             copy = pltpu.make_async_copy(src, dst, in_sem.at[n])
-            copy.start()
+            if n < 7:
+                copy.start()
             ins.append(copy)
         (i_sd, i_cen, i_part, i_cnt, i_pw, i_cin, i_rad, i_refl, i_rd, i_tw, i_fm, i_far) = ins
 
-        def phases(dirs, out):
-            for a in range(2):
-                for b in range(2):
-                    total = None
-                    for d in range(3):
-                        term = dirs[d : d + 1, :] * cen_v[a, b : b + 1, d : d + 1]
-                        total = term if total is None else total + term
-                    out[0, 2 * a + b : 2 * a + b + 1, :] = total
-            phi = out[0, 0:4, :]
-            out[0, 0:4, :] = jnp.cos(phi)
-            out[1, 0:4, :] = jnp.sin(phi)
+        def phases(dirs, out, cen, first):
+            for n in range(4):
+                total = None
+                for d in range(3):
+                    term = dirs[d : d + 1, :] * cen[n // 2, n % 2 : n % 2 + 1, d : d + 1]
+                    total = term if total is None else total + term
+                out[0, first + n : first + n + 1, :] = total
+            phi = out[0, first : first + 4, :]
+            out[0, first : first + 4, :] = jnp.cos(phi)
+            out[1, first : first + 4, :] = jnp.sin(phi)
 
         for d in range(2):
 
             @pl.when(jnp.logical_not(has_x[d]))
             def _():
                 wr_v[d] = jnp.zeros(wr_v.shape[1:], F32)
+                nrefl_v[d] = jnp.zeros(nrefl_v.shape[1:], F32)
+                ncen_v[d] = jnp.zeros(ncen_v.shape[1:], F32)
                 for t in range(2):
                     for g in range(G):
                         pr_v[t, g, d] = jnp.zeros(pr_v.shape[3:], BF16)
 
         i_sd.wait()
         i_cen.wait()
-        phases(sd_v, cs_v)
+        phases(sd_v, cs_v, cen_v, 0)
 
         i_cin.wait()
         for p in range(4):
@@ -151,7 +153,7 @@
             x0 = jnp.dot(x, rad_v[0], preferred_element_type=F32)
             x1 = jnp.dot(x, rad_v[1], preferred_element_type=F32)
             out = []
-            for p in range(4):
+            for p in range(x.shape[0] // 16):
                 r, i = 16 * p, 16 * p + 8
                 out.append((x0[r : r + 8] - x1[i : i + 8], x1[r : r + 8] + x0[i : i + 8]))
             return out
@@ -185,6 +187,19 @@
                 device_id=x_dev(x_nb[d]),
                 device_id_type=MESH,
             )
+
+        def n_copies(d):
+            return [
+                pltpu.make_async_remote_copy(
+                    src_ref=src.at[d],
+                    dst_ref=dst.at[1 - d],
+                    send_sem=n_sem.at[0, n, d],
+                    recv_sem=n_sem.at[1, n, 1 - d],
+                    device_id=x_dev(x_nb[d]),
+                    device_id_type=MESH,
+                )
+                for n, (src, dst) in enumerate(((refl_v, nrefl_v), (cen_v, ncen_v)))
+            ]
 
         def radiate(t, g, x):
             for p, (re, im) in enumerate(spectrum(x)):
@@ -255,7 +270,7 @@
                 s = cs_v[1, p : p + 1, :]
                 both = jnp.concatenate([re * c - im * s, re * s + im * c], axis=0)
                 x_v[16 * p : 16 * p + 16, :] = both.astype(BF16)
-            x = x_v[...]
+            x = x_v[0:64, :]
             q0 = jnp.dot(x, radt_v[0], preferred_element_type=F32)
             q1 = jnp.dot(x, radt_v[1], preferred_element_type=F32)
             for p in range(4):
@@ -268,30 +283,55 @@
                 curf_v[g, 16 * p : 16 * p + 16, :] = new.astype(BF16)
             return curf_v[g]
 
-        def rs_copy(g, d, peer):
+        def rs_copy(n, d, peer):
             return pltpu.make_async_remote_copy(
-                src_ref=sb_v.at[g, peer],
-                dst_ref=rb_v.at[g, d],
-                send_sem=rs_sem.at[0, g],
-                recv_sem=rs_sem.at[1, g],
+                src_ref=sb_v.at[n, peer],
+                dst_ref=rb_v.at[n, d],
+                send_sem=rs_sem.at[0, n],
+                recv_sem=rs_sem.at[1, n],
                 device_id=x_dev(peer),
                 device_id_type=MESH,
             )
 
-        def rs_all(g):
+        def rs_all(n):
             return pltpu.make_async_remote_copy(
-                src_ref=sb_v.at[g, pl.ds(0, n_px - 1)],
-                dst_ref=rb_v.at[g, pl.ds(1, n_px - 1)],
-                send_sem=rs_sem.at[0, g],
-                recv_sem=rs_sem.at[1, g],
+                src_ref=sb_v.at[n, pl.ds(0, n_px - 1)],
+                dst_ref=rb_v.at[n, pl.ds(1, n_px - 1)],
+                send_sem=rs_sem.at[0, n],
+                recv_sem=rs_sem.at[1, n],
                 device_id=x_dev(ring(pi + 1, n_px)),
                 device_id_type=MESH,
             )
 
         def far_field(g):
-            for p, (re, im) in enumerate(spectrum(curf_v[g])):
+            for q in range(8):
+                if q < 4:
+                    total = acc_v[g, 16 * q : 16 * q + 16, :]
+                else:
+                    b = q % 2
+                    total = push_v[1, g, (q - 4) // 2, 16 * b : 16 * b + 16, :].astype(F32)
+                re, im = total[0:8], total[8:16]
+                c = cs_v[0, q : q + 1, :]
+                s = cs_v[1, q : q + 1, :]
+                both = jnp.concatenate([re * c - im * s, re * s + im * c], axis=0)
+                x_v[16 * q : 16 * q + 16, :] = both.astype(BF16)
+            x = x_v[...]
+            q0 = jnp.dot(x, radt_v[0], preferred_element_type=F32)
+            q1 = jnp.dot(x, radt_v[1], preferred_element_type=F32)
+            for q in range(8):
+                r, i = 16 * q, 16 * q + 8
+                got = jnp.concatenate(
+                    [q0[r : r + 8] - q1[i : i + 8], q1[r : r + 8] + q0[i : i + 8]], axis=0
+                )
+                if q < 4:
+                    new = cinc_v[g, 16 * q : 16 * q + 16, :].astype(F32)
+                    new = new + refl_v[q // 2, q % 2 : q % 2 + 1, :] * got
+                else:
+                    new = nrefl_v[(q - 4) // 2, q % 2 : q % 2 + 1, :] * got
+                xf_v[16 * q : 16 * q + 16, :] = new.astype(BF16)
+            for q, (re, im) in enumerate(spectrum(xf_v[...])):
                 both = jnp.concatenate([re, im], axis=0)
-                x_v[16 * p : 16 * p + 16, :] = both.astype(BF16)
+                x_v[16 * q : 16 * q + 16, :] = both.astype(BF16)
             x = x_v[...]
             for n in range(4):
                 beams = jnp.dot(x, far_v[:, 512 * n : 512 * n + 512], preferred_element_type=F32)
@@ -299,7 +339,7 @@
                     u = 4 * n + m
                     at = slice(LN * m, LN * m + LN)
                     far_re = far_im = None
-                    for p in range(4):
+                    for p in range(8):
                         br = beams[16 * p : 16 * p + 8, at]
                         bi = beams[16 * p + 8 : 16 * p + 16, at]
                         c = cv_v[0, p : p + 1, LN * u : LN * u + LN]
@@ -328,12 +368,10 @@
                 fm_v[...], y_v[...], (((1,), (1,)), ((), ())), preferred_element_type=F32
             )
             sb_v[g] = bins.reshape(n_px, rows_p, LN).astype(BF16)
-
-            def send(d, carry):
-                rs_copy(g, d, ring(pi + d, n_px)).start()
-                return carry
-
-            lax.fori_loop(1, n_px, send, 0)
+            for d in range(1, n_px):
+                peer = pi + d
+                peer = jnp.where(peer >= n_px, peer - n_px, peer)
+                rs_copy(g, d, peer).start()
 
         def z_sum_copy(g, owner):
             return pltpu.make_async_remote_copy(
@@ -385,8 +423,16 @@
             def _():
                 w_copy(d).start()
 
-        for g in range(G):
-            radiate(0, g, cinc_v[g])
+        def chunks(body):
+            def step(g, carry):
+                body(g)
+                return carry
+
+            lax.fori_loop(0, G, step, 0)
+
+        chunks(lambda g: radiate(0, g, cinc_v[g]))
+        for copy in ins[7:]:
+            copy.start()
 
         def z_tell(n):
             if n < len(z_rounds):
@@ -422,8 +468,15 @@
         for part in range(2):
             radt_v[part] = rad_v[part].T
         i_refl.wait()
+        for d in range(2):
+
+            @pl.when(has_x[d])
+            def _():
+                for copy in n_copies(d):
+                    copy.start()
+
         i_rd.wait()
-        phases(rd_v, cv_v)
+        phases(rd_v, cv_v, cen_v, 0)
         i_tw.wait()
         i_fm.wait()
         i_far.wait()
@@ -432,44 +485,53 @@
             @pl.when(has_x[d])
             def _():
                 w_copy(1 - d).wait_recv()
-
+                for copy in n_copies(1 - d):
+                    copy.wait_recv()
+
+        phases(sd_v, cs_v, ncen_v, 4)
+        phases(rd_v, cv_v, ncen_v, 4)
         x_hear(0)
         x_tell(1)
-        for g in range(G):
-            partner_sums(0, g)
+        chunks(lambda g: partner_sums(0, g))
         x_hear(1)
         x_tell(2)
         z_hear(0)
         z_tell(1)
-        for g in range(G):
+        def first_receive(g):
             radiate(1, g, receive(0, g))
-        x_hear(2)
-        x_tell(3)
+
+            @pl.when(g == 1)
+            def _():
+                x_hear(2)
+                x_tell(3)
+
+        chunks(first_receive)
+        x_hear(3)
+        x_tell(4)
         z_hear(1)
         z_tell(2)
-        for g in range(G):
+
+        def second_bounce(g):
             partner_sums(1, g)
-            if g == 0:
-                x_hear(3)
-                x_tell(4)
-        for g in range(G):
-            receive(1, g)
-            if g == 0:
+
+            @pl.when(g == 0)
+            def _():
                 x_hear(4)
+
             far_field(g)
+
+        chunks(second_bounce)
+        chunks(lambda g: receive(1, g))
         z_hear(2)
-        for p in range(4):
+        def assemble(p, carry):
+            pieces = [curf_v[g, pl.ds(pl.multiple_of(16 * p, 16), 16), :].astype(F32) for g in range(G)]
             for part in range(2):
-                whole = jnp.concatenate(
-                    [
-                        curf_v[g, 16 * p : 16 * p + 16, :].astype(F32)[8 * part : 8 * part + 8]
-                        for g in range(G)
-                    ],
-                    axis=0,
-                )
+                whole = jnp.concatenate([x[8 * part : 8 * part + 8] for x in pieces], axis=0)
                 cur_o[p // 2, p % 2, part] = whole.astype(BF16)
-        for g in range(G):
-            gather_bins(g)
+            return carry
+
+        lax.fori_loop(0, 4, assemble, 0)
+        chunks(gather_bins)
 
         for t in range(2):
             for g in range(G):
@@ -480,6 +542,8 @@
             @pl.when(has_x[d])
             def _():
                 w_copy(d).wait_send()
+                for copy in n_copies(d):
+                    copy.wait_send()
                 for t in range(2):
                     for g in range(G):
                         x_copy(t, g, d).wait_send()
@@ -520,6 +584,17 @@
     return kernel
 
 
+def hand_over(cur_i, img_i, cur_o, img_o, sem):
+    copies = [
+        pltpu.make_async_copy(cur_i, cur_o, sem.at[0]),
+        pltpu.make_async_copy(img_i, img_o, sem.at[1]),
+    ]
+    for copy in copies:
+        copy.start()
+    for copy in copies:
+        copy.wait()
+
+
 def tables(n_px):
     qp = LN // n_px
     row = np.arange(2 * LN)
@@ -564,10 +639,12 @@
             V((2, TW, LN), F32),
             V((64, LN), F32),
             V((2, 32, LN), F32),
+            V((2, 2, units), F32),
+            V((2, 2, 3), F32),
             V((2, 8, dirs), F32),
             V((2, 8, rcv), F32),
             V((G, 64, units), BF16),
-            V((64, units), BF16),
+            V((128, units), BF16),
             V((2, G, 64, dirs), BF16),
             V((2, G, 2, 64, dirs), BF16),
             V((G, 64, dirs), F32),
@@ -575,6 +652,7 @@
             V((2, G, 2, 32, dirs), BF16),
             V((G, 64, units), BF16),
             V((2, TW, KC, LN), F32),
+            V((128, units), BF16),
             V((LN, 2 * LN), BF16),
             V((G, n_px, 2 * qp, LN), BF16),
             V((G, n_px, 2 * qp, LN), BF16),
@@ -582,6 +660,7 @@
             V((n_z, 2 * qp, LN), BF16),
             dma((12,)),
             dma((2, 2)),
+            dma((2, 2, 2)),
             dma((2, 2, G, 2)),
             dma((2, 2, G, 2)),
             dma((2, G)),
@@ -589,7 +668,7 @@
             regular((max(1, len(doubling(n_z // 2))),)),
             regular((max(1, len(doubling(n_px - 1))),)),
         ]
-        return pl.pallas_call(
+        results = pl.pallas_call(
             kernel,
             out_shape=(
                 pltpu.VMEM(cin.shape, BF16),
@@ -608,6 +687,17 @@
             cin, rad, far, refl, jnp.transpose(cen, (1, 2, 0)), sd, rd, part, cnt, pw,
             jnp.asarray(second, BF16), jnp.asarray(twiddle),
         )
+        return pl.pallas_call(
+            hand_over,
+            out_shape=(
+                jax.ShapeDtypeStruct(cin.shape, BF16),
+                jax.ShapeDtypeStruct((kz, TW * qp), F32),
+            ),
+            in_specs=[pl.BlockSpec(memory_space=pl.ANY)] * 2,
+            out_specs=(pl.BlockSpec(memory_space=pl.ANY), pl.BlockSpec(memory_space=pl.ANY)),
+            scratch_shapes=[dma((2,))],
+            compiler_params=pltpu.CompilerParams(vmem_limit_bytes=1 << 20),
+        )(*results)
 
     in_specs = (
         P("px", "py", None, None, None),

time: 47 us -> 44.3 us (0.943)
  Pallas kernels: 44.9 us -> 43.2 us
  local copies, waits for them, and re-layouts: 1.27 us -> 0 us
    pallas_call x1, Pallas kernels: 44.9 us -> 42.5 us  [local(): pl.pallas_call(kernel, out_shape=(pltpu.VMEM(cin.shape, BF16), pltpu.VMEM...]
    unnamed x2 -> x0, local copies, waits for them, and re-layouts: 1.27 us -> none
    pallas_call x0 -> x1, Pallas kernels: none -> 0.72 us  [local(): pl.pallas_call(hand_over, out_shape=(jax.ShapeDtypeStruct(cin.shape, BF16...]
where the time goes in v3:
time: 44.3 us; the launch traced here: 43.8 us
  Pallas kernels  43.2 us (98%)
  between operations  0.64 us (1%)
    pallas_call x1, Pallas kernels, local(): pl.pallas_call(kernel, out_shape=(pltpu.VMEM(cin.shape, BF16), pltpu.VMEM...  42.5 us

profile of v3, /device:TPU:1, one launch (start us, length us, event | category | flops | bytes accessed | tf_op | source)
XLA Modules:
  0.0 43.8 jit_solution(7884747317367763332)
XLA Ops:
  0.6 42.5 %shard_map.131 = (bf16[2,2,2,32,512]{4,3,2,1,0:T(8,128)(2,1)S(1)}, f32[2,64]{1,0:T(2,128)S(1)}) custom-call(bf16[2,2,2,32,512]{4,3,2,1,0:T(8,128)(2,1)} %cin_h.1, bf16[2,512,512]{2,1,0:T(8,128)(2,1)} %rad_h.1, bf16[512,2048]{1,0:T(8,128)(2,1)} %far_h.1, f32[2,2,512]{2,1,0:T(2,128)} %refl_h.1, f32[2,2,3]{2,1,0:T(2,128)} %bitcast.1, f32[3,512]{1,0:T(4,128)} %sd_h.1, ...), custom_call_target="tpu_custom_call" | custom-call | tf_op jit(solution)/shard_map/pallas_call | solution.py:671
  43.1 0.7 %shard_map.132 = (bf16[2,2,2,32,512]{4,3,2,1,0:T(8,128)(2,1)}, f32[2,64]{1,0:T(2,128)}) custom-call(bf16[2,2,2,32,512]{4,3,2,1,0:T(8,128)(2,1)S(1)} %get-tuple-element.4.cur_i, f32[2,64]{1,0:T(2,128)S(1)} %get-tuple-element.5.img_i), custom_call_target="tpu_custom_call" | custom-call | tf_op jit(solution)/shard_map/pallas_call | solution.py:690

commit v4 on v3

--- a/solution.py
+++ b/solution.py
@@ -423,12 +423,12 @@
             def _():
                 w_copy(d).start()
 
-        def chunks(body):
+        def chunks(body, first=0, last=G):
             def step(g, carry):
                 body(g)
                 return carry
 
-            lax.fori_loop(0, G, step, 0)
+            lax.fori_loop(first, last, step, 0)
 
         chunks(lambda g: radiate(0, g, cinc_v[g]))
         for copy in ins[7:]:
@@ -521,8 +521,10 @@
             far_field(g)
 
         chunks(second_bounce)
-        chunks(lambda g: receive(1, g))
+        chunks(lambda g: receive(1, g), 0, G // 2)
         z_hear(2)
+        gather_bins(0)
+        chunks(lambda g: receive(1, g), G // 2, G)
         def assemble(p, carry):
             pieces = [curf_v[g, pl.ds(pl.multiple_of(16 * p, 16), 16), :].astype(F32) for g in range(G)]
             for part in range(2):
@@ -531,7 +533,7 @@
             return carry
 
         lax.fori_loop(0, 4, assemble, 0)
-        chunks(gather_bins)
+        chunks(gather_bins, 1, G)
 
         for t in range(2):
             for g in range(G):

time: 44.3 us -> 42.6 us (0.962)
  Pallas kernels: 43.2 us -> 41.8 us
    pallas_call x1, Pallas kernels: 42.5 us -> 41.1 us  [local(): pl.pallas_call(kernel, out_shape=(pltpu.VMEM(cin.shape, BF16), pltpu.VMEM...]
where the time goes in v4:
time: 42.6 us; the launch traced here: 42.4 us
  Pallas kernels  41.8 us (98%)
  between operations  0.64 us (2%)
    pallas_call x1, Pallas kernels, local(): pl.pallas_call(kernel, out_shape=(pltpu.VMEM(cin.shape, BF16), pltpu.VMEM...  41.1 us

profile of v4, /device:TPU:1, one launch (start us, length us, event | category | flops | bytes accessed | tf_op | source)
XLA Modules:
  0.0 42.4 jit_solution(5312561636514546640)
XLA Ops:
  0.6 41.1 %shard_map.131 = (bf16[2,2,2,32,512]{4,3,2,1,0:T(8,128)(2,1)S(1)}, f32[2,64]{1,0:T(2,128)S(1)}) custom-call(bf16[2,2,2,32,512]{4,3,2,1,0:T(8,128)(2,1)} %cin_h.1, bf16[2,512,512]{2,1,0:T(8,128)(2,1)} %rad_h.1, bf16[512,2048]{1,0:T(8,128)(2,1)} %far_h.1, f32[2,2,512]{2,1,0:T(2,128)} %refl_h.1, f32[2,2,3]{2,1,0:T(2,128)} %bitcast.1, f32[3,512]{1,0:T(4,128)} %sd_h.1, ...), custom_call_target="tpu_custom_call" | custom-call | tf_op jit(solution)/shard_map/pallas_call | solution.py:673
  41.7 0.7 %shard_map.132 = (bf16[2,2,2,32,512]{4,3,2,1,0:T(8,128)(2,1)}, f32[2,64]{1,0:T(2,128)}) custom-call(bf16[2,2,2,32,512]{4,3,2,1,0:T(8,128)(2,1)S(1)} %get-tuple-element.4.cur_i, f32[2,64]{1,0:T(2,128)S(1)} %get-tuple-element.5.img_i), custom_call_target="tpu_custom_call" | custom-call | tf_op jit(solution)/shard_map/pallas_call | solution.py:692

commit v5 on v4

--- a/solution.py
+++ b/solution.py
@@ -525,6 +525,7 @@
         z_hear(2)
         gather_bins(0)
         chunks(lambda g: receive(1, g), G // 2, G)
+        gather_bins(1)
         def assemble(p, carry):
             pieces = [curf_v[g, pl.ds(pl.multiple_of(16 * p, 16), 16), :].astype(F32) for g in range(G)]
             for part in range(2):
@@ -533,7 +534,7 @@
             return carry
 
         lax.fori_loop(0, 4, assemble, 0)
-        chunks(gather_bins, 1, G)
+        chunks(gather_bins, 2, G)
 
         for t in range(2):
             for g in range(G):

time: 42.6 us -> 42.6 us (level)
  no operation moved by 1% of the time
where the time goes in v5:
time: 42.6 us; the launch traced here: 42.4 us
  Pallas kernels  41.8 us (98%)
  between operations  0.64 us (2%)
    pallas_call x1, Pallas kernels, local(): pl.pallas_call(kernel, out_shape=(pltpu.VMEM(cin.shape, BF16), pltpu.VMEM...  41.1 us

profile of v5, /device:TPU:1, one launch (start us, length us, event | category | flops | bytes accessed | tf_op | source)
XLA Modules:
  0.0 42.4 jit_solution(4340408226090872633)
XLA Ops:
  0.6 41.1 %shard_map.131 = (bf16[2,2,2,32,512]{4,3,2,1,0:T(8,128)(2,1)S(1)}, f32[2,64]{1,0:T(2,128)S(1)}) custom-call(bf16[2,2,2,32,512]{4,3,2,1,0:T(8,128)(2,1)} %cin_h.1, bf16[2,512,512]{2,1,0:T(8,128)(2,1)} %rad_h.1, bf16[512,2048]{1,0:T(8,128)(2,1)} %far_h.1, f32[2,2,512]{2,1,0:T(2,128)} %refl_h.1, f32[2,2,3]{2,1,0:T(2,128)} %bitcast.1, f32[3,512]{1,0:T(4,128)} %sd_h.1, ...), custom_call_target="tpu_custom_call" | custom-call | tf_op jit(solution)/shard_map/pallas_call | solution.py:674
  41.7 0.7 %shard_map.132 = (bf16[2,2,2,32,512]{4,3,2,1,0:T(8,128)(2,1)}, f32[2,64]{1,0:T(2,128)}) custom-call(bf16[2,2,2,32,512]{4,3,2,1,0:T(8,128)(2,1)S(1)} %get-tuple-element.4.cur_i, f32[2,64]{1,0:T(2,128)S(1)} %get-tuple-element.5.img_i), custom_call_target="tpu_custom_call" | custom-call | tf_op jit(solution)/shard_map/pallas_call | solution.py:693
